TPU v7x, 256 devices: a whole 4x4x8 slice. The times are simulated.
256 devices in a mesh: lat: 64 (over z, x, y_hi), lon: 4 (over y_lo, core).
Axes of the slice: x: 4, y: 4 (y_hi: 2, y_lo: 2; y = y_hi * 2 + y_lo), z: 8, core: 2. Of those that a mesh axis runs over, the one named last changes fastest.
Arguments:
- tracers: float32 [4, 8, 256, 5760], P(None, None, 'lat', 'lon'), may hold values from -6 to 6
- merid_courant: float32 [8, 256, 5760], P(None, 'lat', 'lon'), may hold values from -0.45 to 0.45
- zonal_shift: int32 [8, 256], P(None, 'lat'), may hold values from 0 to 64, as said below
- zonal_fraction: float32 [8, 256], P(None, 'lat'), may hold values from 0 to 1
- cutoff: int32 [256], replicated, may hold values from 1 to 1023
- damping: float32 [256], replicated, may hold values from 0.1 to 0.6
Outputs:
- tracer_out: float32 [4, 8, 256, 5760], P(None, None, 'lat', 'lon')
Inputs may be any that keep to these rules, and one draw needn't show every extreme that they name: `zonal_shift`: in row j no displacement exceeds 1 + (64 * |2j - 255|) // 256, a limit that grows toward the poles; below it the values are random.
All inputs are finite; a program needn't handle non-finite values.
Results may differ from a plain program's by a relative error of at most 0.00005.
Values sent between devices are 32-bit elements; how exact they have to be, the bound alone decides.
A program may use at most 64 MiB of HBM per device.

v0:
```python
import math

import jax
import jax.numpy as jnp
from jax import lax
from jax.sharding import PartitionSpec as P

MODES = 1024
SMAX = 64


def passed_along(block, axis, distance):
    devices = range(lax.axis_size(axis))
    route = [(i - distance, i) for i in devices if i - distance in devices]
    return lax.ppermute(block, axis, route)


def passed_along_2(value, axis, steps):
    count = lax.axis_size(axis)
    pairs = [(source, (source + steps) % count) for source in range(count)]
    return lax.ppermute(value, axis, pairs)


def make_basis(columns, wavenumber, lon_cells):
    phase_index = columns[:, None] * wavenumber[None, :] % lon_cells
    angles = phase_index.astype(jnp.float32) * (2.0 * math.pi / lon_cells)
    return jnp.concatenate([jnp.cos(angles), jnp.sin(angles)], axis=1)


def body(tracers, merid_courant, zonal_shift, zonal_fraction, cutoff, damping):
    tracer_count, level_count, row_count, column_count = tracers.shape
    lat_count = lax.axis_size("lat")
    lat_index = lax.axis_index("lat")
    lon_count = lax.axis_size("lon")
    lon_index = lax.axis_index("lon")
    lat_rows = row_count * lat_count
    lon_cells = column_count * lon_count
    below_row = passed_along(tracers[:, :, row_count - 1 :], "lat", 1)
    stacked_edge = jnp.concatenate([tracers[:, :, :1], merid_courant[None, :, :1]], axis=0)
    above_row = passed_along(stacked_edge, "lat", -1)
    face_speed = jnp.concatenate([merid_courant, above_row[tracer_count]], axis=1)
    south_cells = jnp.concatenate([below_row, tracers], axis=2)
    north_cells = jnp.concatenate([tracers, above_row[:tracer_count]], axis=2)
    face_flux = (
        jnp.maximum(face_speed, 0.0)[None] * south_cells
        + jnp.minimum(face_speed, 0.0)[None] * north_cells
    )
    face_row = lat_index * row_count + jnp.arange(row_count + 1, dtype=jnp.int32)
    open_face = (face_row > 0) & (face_row < lat_rows)
    face_flux = jnp.where(open_face[None, None, :, None], face_flux, 0.0)
    advected = tracers + face_flux[:, :, :-1] - face_flux[:, :, 1:]
    rim_width = SMAX + 1
    west_rim = passed_along_2(advected[:, :, :, column_count - rim_width :], "lon", 1)
    extended = jnp.concatenate([west_rim, advected], axis=3)
    moved = extended
    shift_grid = zonal_shift[None, :, :, None]
    for bit_level in range(SMAX.bit_length()):
        stride = 1 << bit_level
        padding = jnp.zeros(moved.shape[:3] + (stride,), moved.dtype)
        pushed = jnp.concatenate([padding, moved[:, :, :, :-stride]], axis=3)
        selected = shift_grid >> bit_level & 1 == 1
        moved = jnp.where(selected, pushed, moved)
    current = moved[:, :, :, rim_width : rim_width + column_count]
    earlier = moved[:, :, :, rim_width - 1 : rim_width - 1 + column_count]
    fraction_here = zonal_fraction[None, :, :, None]
    shifted = (1.0 - fraction_here) * current + fraction_here * earlier
    wavenumber = jnp.arange(MODES, dtype=jnp.int32)
    local_columns = lon_index * column_count + jnp.arange(column_count, dtype=jnp.int32)
    scale_mode = jnp.where(wavenumber == 0, 1.0, 2.0).astype(jnp.float32) / lon_cells
    quarter = lat_count // 4
    is_cap = (lat_index < quarter) | (lat_index >= lat_count - quarter)
    row_base = lat_index * row_count
    cut_rows = lax.dynamic_slice_in_dim(cutoff, row_base, row_count)
    damp_rows = lax.dynamic_slice_in_dim(damping, row_base, row_count)
    weight = jnp.where(wavenumber[None, :] <= cut_rows[:, None], scale_mode[None, :], 0.0)
    weight = jnp.concatenate([weight, weight], axis=1)
    flat_rows = shifted.reshape(-1, column_count)
    basis_table = make_basis(local_columns, wavenumber, lon_cells)
    coeffs = jnp.dot(
        flat_rows, basis_table, precision=lax.Precision.HIGHEST, preferred_element_type=jnp.float32
    )
    coeffs = lax.psum(coeffs, "lon")
    coeffs = (
        coeffs.reshape(shifted.shape[0], level_count, row_count, 2 * MODES) * weight[None, None]
    )
    low_part = jnp.dot(
        coeffs.reshape(-1, 2 * MODES),
        basis_table.T,
        precision=lax.Precision.HIGHEST,
        preferred_element_type=jnp.float32,
    )
    low_part = low_part.reshape(shifted.shape)
    damp_factor = damp_rows[None, None, :, None]
    filtered = damp_factor * shifted + (1.0 - damp_factor) * low_part
    result = jnp.where(is_cap, filtered, shifted)
    return result


def solution(mesh):
    placed = (
        P(None, None, "lat", "lon"),
        P(None, "lat", "lon"),
        P(None, "lat"),
        P(None, "lat"),
        P(),
        P(),
    )
    return jax.shard_map(
        body, mesh=mesh, in_specs=placed, out_specs=P(None, None, "lat", "lon"), check_vma=False
    )
```

profile of v0, /device:TPU:1, one launch (start us, length us, event | category | flops | bytes accessed | tf_op | source)
XLA Modules:
  0.0 144.0 jit_solution(4314243919755971988)
XLA Ops:
  6.5 0.0 all-reduce.9.cloned.1.call-start
  6.5 1.4 copy.36
  8.0 1.0 copy.32
  9.0 1.3 collective-permute-start
  10.3 6.3 %collective-permute-start.1 = (f32[4,8,1,1440]{3,1,2,0:T(8,128)S(1)}, f32[4,8,1,1440]{3,1,2,0:T(8,128)S(1)}, u32[]{:S(2)}, u32[]{:S(2)}) collective-permute-start(f32[4,8,1,1440]{3,1,2,0:T(8,128)S(1)} %get-tuple-element.8), channel_id=1, source_target_pairs={{0,4},{4,8},{8,12},{12,16},{16,20},{20,24},{24,28},{28,32},{32,36}... | collective-permute-start | bytes 552968 | tf_op jit(solution)/shard_map/ppermute | solution.py:15
  16.6 0.0 copy-start.2
  16.6 0.0 copy-start
  16.6 27.2 %fusion.8 = (f32[1440,1024]{1,0:T(8,128)}, f32[1440,1024]{1,0:T(8,128)}) fusion(s32[1440]{0:T(1024)S(1)} %iota_add_fusion), kind=kLoop, calls=%fused_computation.11 | loop fusion | flops 13271040 | bytes 11802240 | tf_op jit(solution)/shard_map/cos | solution.py:27
  43.8 0.0 copy-start.1
  43.8 0.0 copy-done.2
  43.9 0.0 collective-permute-done
  43.9 0.0 collective-permute-done.1
  44.0 0.2 fusion.21
  44.2 0.0 copy-done
  44.2 0.4 slice_subtract_fusion
  44.6 0.1 slice.75
  44.7 2.7 %collective-permute-start.2 = (f32[4,8,4,65]{3,1,2,0:T(8,128)S(1)}, f32[4,8,4,65]{3,1,2,0:T(8,128)S(1)}, u32[]{:S(2)}, u32[]{:S(2)}) collective-permute-start(f32[4,8,4,65]{3,1,2,0:T(8,128)S(1)} %slice.75), channel_id=1, source_target_pairs={{0,1},{1,2},{2,3},{3,0},{4,5},{5,6},{6,7},{7,4},{8,9},{9,10},{10,1... | collective-permute-start | bytes 99848 | tf_op jit(solution)/shard_map/ppermute | solution.py:21
  47.4 0.0 copy-done.1
  47.4 1.3 collective-permute-done.2
  48.7 0.3 fusion.23
  49.0 0.5 fusion.22
  49.4 0.3 pad_select_fusion.5
  49.7 0.3 pad_select_fusion.4
  50.0 0.3 pad_select_fusion.3
  50.3 0.3 pad_select_fusion.2
  50.6 0.3 pad_select_fusion.1
  50.8 0.3 pad_select_fusion
  51.1 0.5 fusion.24
  51.6 0.5 copy.37
  52.1 0.3 reshape.91
  52.4 0.0 copy-start.4
  52.4 0.0 copy-start.3
  52.4 11.9 %fusion.2 = f32[128,2048]{1,0:T(8,128)} fusion(f32[128,1440]{1,0:T(8,128)S(1)} %reshape.91, f32[1440,1024]{1,0:T(8,128)} %get-tuple-element.12, f32[1440,1024]{1,0:T(8,128)} %get-tuple-element.11), kind=kOutput, calls=%fused_computation.3 | convolution fusion | flops 4532797440 | bytes 13582336 | tf_op jit(solution)/shard_map/dot_general | solution.py:79
  64.3 0.0 all-reduce.9.cloned.1.call-update
  64.3 0.0 copy-done.4
  64.4 0.1 dynamic_slice.7
  64.4 0.1 fusion.27
  64.5 0.2 mul.103
  64.8 0.4 mul.104
  65.1 0.0 copy-done.3
  65.2 0.1 broadcast_subtract_fusion.1
  65.2 52.3 %all-reduce.9.cloned.1.call-done = f32[128,2048]{1,0:T(8,128)} async-done(((f32[128,2048]{1,0:T(8,128)}), f32[128,2048]{1,0:T(8,128)}) %all-reduce.9.cloned.1.call-update) | async-done | bytes 1048592 | tf_op jit(solution)/shard_map/psum | solution.py:82
  117.6 1.3 mul.105
  118.9 0.3 dot_general.9
  119.2 16.6 %fusion.16 = f32[4,8,4,1440]{3,1,2,0:T(8,128)S(1)} fusion(f32[4,8,4,1440]{3,1,2,0:T(8,128)S(1)} %fusion.24, f32[1440,1024]{1,0:T(8,128)} %get-tuple-element.12, f32[1440,1024]{1,0:T(8,128)} %get-tuple-element.11, f32[4,8,4,2048]{3,2,1,0:T(4,128)S(1)} %dot_general.9, f32[4]{0:T(128)S(1)} %get-tuple-element.5, f32[4]{0:T(128)S(1)} %get-tuple-element.6, ...), kind=kOutput, calls=%fused_computation.15 | convolution fusion | flops 4533534720 | bytes 14319649 | tf_op jit(solution)/shard_map/dot_general | solution.py:86
  135.8 1.4 copy.39
  (12 shorter events, 0.1 us)
Async XLA Ops:
  6.5 111.0 %all-reduce.9.cloned.1.call-start = ((), (), s32[]{:S(2)}) async-start(), calls=%async_computation | async-start | bytes 2097152 | tf_op jit(solution)/shard_map/psum | solution.py:82
  9.0 34.9 %collective-permute-start = (f32[5,8,1,1440]{3,1,2,0:T(8,128)S(1)}, f32[5,8,1,1440]{3,1,2,0:T(8,128)S(1)}, u32[]{:S(2)}, u32[]{:S(2)}) collective-permute-start(f32[5,8,1,1440]{3,1,2,0:T(8,128)S(1)} %pad_maximum_fusion.4), channel_id=1, source_target_pairs={{4,0},{8,4},{12,8},{16,12},{20,16},{24,20},{28,24},{32,28},{36,32}... | collective-permute-start | bytes 691208 | tf_op jit(solution)/shard_map/ppermute | solution.py:15
  10.3 33.7 %collective-permute-start.1 = (f32[4,8,1,1440]{3,1,2,0:T(8,128)S(1)}, f32[4,8,1,1440]{3,1,2,0:T(8,128)S(1)}, u32[]{:S(2)}, u32[]{:S(2)}) collective-permute-start(f32[4,8,1,1440]{3,1,2,0:T(8,128)S(1)} %get-tuple-element.8), channel_id=1, source_target_pairs={{0,4},{4,8},{8,12},{12,16},{16,20},{20,24},{24,28},{28,32},{32,36}... | collective-permute-start | bytes 552968 | tf_op jit(solution)/shard_map/ppermute | solution.py:15
  16.6 27.2 %copy-start.2 = (s32[8,4]{0,1:T(4,128)S(1)}, s32[8,4]{0,1:T(4,128)}, u32[]{:S(2)}) copy-start(s32[8,4]{0,1:T(4,128)} %param.8) | copy-start | bytes 388
  16.6 27.6 %copy-start = (f32[4,8,4,1440]{3,2,1,0:T(4,128)S(1)}, f32[4,8,4,1440]{3,2,1,0:T(4,128)}, u32[]{:S(2)}) copy-start(f32[4,8,4,1440]{3,2,1,0:T(4,128)} %param.6) | copy-start | bytes 2211844
  43.8 3.5 %copy-start.1 = (f32[8,4]{0,1:T(4,128)S(1)}, f32[8,4]{0,1:T(4,128)}, u32[]{:S(2)}) copy-start(f32[8,4]{0,1:T(4,128)} %param.9) | copy-start | bytes 388
  44.7 4.0 %collective-permute-start.2 = (f32[4,8,4,65]{3,1,2,0:T(8,128)S(1)}, f32[4,8,4,65]{3,1,2,0:T(8,128)S(1)}, u32[]{:S(2)}, u32[]{:S(2)}) collective-permute-start(f32[4,8,4,65]{3,1,2,0:T(8,128)S(1)} %slice.75), channel_id=1, source_target_pairs={{0,1},{1,2},{2,3},{3,0},{4,5},{5,6},{6,7},{7,4},{8,9},{9,10},{10,1... | collective-permute-start | bytes 99848 | tf_op jit(solution)/shard_map/ppermute | solution.py:21
  52.4 11.9 %copy-start.4 = (s32[256]{0:T(256)S(1)}, s32[256]{0:T(256)}, u32[]{:S(2)}) copy-start(s32[256]{0:T(256)} %param.10) | copy-start | bytes 3076
  52.4 12.7 %copy-start.3 = (f32[256]{0:T(256)S(1)}, f32[256]{0:T(256)}, u32[]{:S(2)}) copy-start(f32[256]{0:T(256)} %param.11) | copy-start | bytes 3076
Sparse Core Ops, SparseCore 0:
  64.5 53.0 all-reduce.8
where the time goes:
time: 144 us
  waiting for transfers between devices  53.7 us (37%)
  other arithmetic  32.3 us (22%)
  matrix products  28.4 us (20%)
  between operations  13.7 us (10%)
  starting transfers between devices  10.3 us (7%)
  local copies, waits for them, and re-layouts  5.68 us (4%)
    psum x1, waiting for transfers between devices, body(): coeffs = lax.psum(coeffs, 'lon')  52.3 us
    cos x1, other arithmetic, make_basis(): return jnp.concatenate([jnp.cos(angles), jnp.sin(angles)], axis=1)  27.2 us
    dot_general x1, matrix products, body(): jnp.dot(coeffs.reshape(-1, 2 * MODES), basis_table.T, precision=lax.Preci...  16.6 us
    dot_general x1, matrix products, body(): jnp.dot(flat_rows, basis_table, precision=lax.Precision.HIGHEST, preferre...  11.9 us
    ppermute x2, starting transfers between devices, passed_along(): return lax.ppermute(block, axis, route)  7.57 us
  transfers between devices with their start and end apart: 4, of which 2 were waited for; matrix products, arithmetic and copies ran while one was open for 20% of the time, Pallas kernels for 0%

commit v1 on v0

v1 whole, which is shorter than its diff:
```python
import functools
import math

import jax
import jax.numpy as jnp
import numpy as np
from jax import lax
from jax.experimental import pallas as pl
from jax.experimental.pallas import tpu as pltpu
from jax.sharding import PartitionSpec as P

MODES = 1024
LANES = 128
PTS = 45
HALF = 23
SPAN = 23
MESH = pl.DeviceIdType.MESH


def residues():
    found = []
    for k5 in range(3):
        for k9 in range(5 if k5 == 0 else 9):
            kk = next(k for k in range(PTS) if k % 5 == k5 and k % 9 == k9)
            found.append(kk if kk <= PTS // 2 else kk - PTS)
    return found


def tables(lon_cells):
    res = np.array(residues(), np.int64)
    lane = np.arange(LANES, dtype=np.int64)
    ang = (res[:, None] * lane[None, :] % lon_cells) * (2 * math.pi / lon_cells)
    twid = np.stack([np.cos(ang), np.sin(ang)]).astype(np.float32)
    half = LANES // 2
    k2 = np.zeros(LANES, np.int64)
    valid = np.zeros(LANES, bool)
    for part in range(2):
        k2[part * half : part * half + 2 * SPAN + 1] = np.arange(-SPAN, SPAN + 1)
        valid[part * half : part * half + 2 * SPAN + 1] = True
    mode = res[:, None] + PTS * k2[None, :]
    kabs = np.abs(mode)
    keep = valid[None, :] & (kabs < MODES) & ~((res[:, None] == 0) & (mode < 0))
    kabs = np.where(keep, kabs, 1 << 20).astype(np.int32)
    scale = np.where(mode == 0, 1.0, 2.0) / lon_cells
    scale = np.where(keep, scale, 0.0).astype(np.float32)
    ang2 = (k2[None, :] * lane[:, None] % LANES) * (2 * math.pi / LANES)
    c2 = np.cos(ang2) * valid[None, :]
    s2 = np.sin(ang2) * valid[None, :]
    first = np.arange(LANES) < half
    fwd = np.concatenate(
        [np.where(first, c2, -s2), np.where(first, s2, c2)], axis=0
    )
    inv = np.concatenate(
        [np.where(first, c2, -s2), np.where(first, s2, c2)], axis=0
    ).T
    return twid, kabs, scale, fwd.astype(np.float32), inv.astype(np.float32)


def halves(table):
    high = jnp.asarray(table).astype(jnp.bfloat16)
    low = (jnp.asarray(table) - high.astype(jnp.float32)).astype(jnp.bfloat16)
    return high, low


def split_dot(value, high, low):
    vh = value.astype(jnp.bfloat16)
    vl = (value - vh.astype(jnp.float32)).astype(jnp.bfloat16)
    dot = functools.partial(jnp.dot, preferred_element_type=jnp.float32)
    return dot(vh, high) + (dot(vl, high) + dot(vh, low))


def cs(count, turn):
    return math.cos(2 * math.pi * turn / count), math.sin(2 * math.pi * turn / count)


def real5(x):
    e1, o1, e2, o2 = x[1] + x[4], x[1] - x[4], x[2] + x[3], x[2] - x[3]
    c1, s1 = cs(5, 1)
    c2, s2 = cs(5, 2)
    return (
        x[0] + (e1 + e2),
        (x[0] + (c1 * e1 + c2 * e2), -(s1 * o1 + s2 * o2)),
        (x[0] + (c2 * e1 + c1 * e2), s1 * o2 - s2 * o1),
    )


def total(terms):
    while len(terms) > 1:
        terms = [sum(terms[i : i + 2][1:], terms[i]) for i in range(0, len(terms), 2)]
    return terms[0]


def real9(x):
    e = [x[j] + x[9 - j] for j in range(1, 5)]
    o = [x[j] - x[9 - j] for j in range(1, 5)]
    out = [(total([x[0]] + e), None)]
    for k in range(1, 5):
        re = total([x[0]] + [cs(9, j * k)[0] * e[j - 1] for j in range(1, 5)])
        im = total([-cs(9, j * k)[1] * o[j - 1] for j in range(1, 5)])
        out.append((re, im))
    return out


def complex9(re, im, sign):
    er = [re[j] + re[9 - j] for j in range(1, 5)]
    ei = [im[j] + im[9 - j] for j in range(1, 5)]
    dr = [re[j] - re[9 - j] for j in range(1, 5)]
    di = [im[j] - im[9 - j] for j in range(1, 5)]
    out = [None] * 9
    out[0] = (total([re[0]] + er), total([im[0]] + ei))
    for k in range(1, 5):
        c = [cs(9, j * k)[0] for j in range(1, 5)]
        s = [sign * cs(9, j * k)[1] for j in range(1, 5)]
        pr = total([re[0]] + [c[j] * er[j] for j in range(4)])
        pi = total([im[0]] + [c[j] * ei[j] for j in range(4)])
        qr = total([s[j] * di[j] for j in range(4)])
        qi = total([s[j] * dr[j] for j in range(4)])
        out[k] = (pr - qr, pi + qi)
        out[9 - k] = (pr + qr, pi - qi)
    return out


def forward45(x):
    zero, one, two = [], [], []
    for p9 in range(9):
        a0, a1, a2 = real5([x[(9 * p5 + 5 * p9) % PTS] for p5 in range(5)])
        zero.append(a0)
        one.append(a1)
        two.append(a2)
    out = real9(zero)
    for part in (one, two):
        out += complex9([a[0] for a in part], [a[1] for a in part], -1.0)
    return out


def inverse45(v):
    zero, one, two = v[:5], v[5:14], v[14:]
    b0 = [None] * 9
    b0[0] = total([z[0] for z in zero])
    for p in range(1, 5):
        pr = total([zero[0][0]] + [cs(9, p * k)[0] * zero[k][0] for k in range(1, 5)])
        qr = total([cs(9, p * k)[1] * zero[k][1] for k in range(1, 5)])
        b0[p] = pr - qr
        b0[9 - p] = pr + qr
    b1 = complex9([a[0] for a in one], [a[1] for a in one], 1.0)
    b2 = complex9([a[0] for a in two], [a[1] for a in two], 1.0)
    c1, s1 = cs(5, 1)
    c2, s2 = cs(5, 2)
    out = [None] * PTS
    for p9 in range(9):
        (r1, i1), (r2, i2), base = b1[p9], b2[p9], b0[p9]
        ca = base + (c1 * r1 + c2 * r2)
        sa = s1 * i1 + s2 * i2
        cb = base + (c2 * r1 + c1 * r2)
        sb = s2 * i1 - s1 * i2
        vals = [base + (r1 + r2), ca - sa, cb - sb, cb + sb, ca + sa]
        for p5 in range(5):
            out[(9 * p5 + 5 * p9) % PTS] = vals[p5]
    return out


def compute_kernel(
    tr, cour, south, north_t, north_c, shift, frac, cut, damp, open_s, open_n, cap,
    twid, kabs, scale, fwd_h, fwd_l, inv_h, inv_l, out,
    line, moved, spec, wave,
):
    tracer_count = tr.shape[1]
    columns = tr.shape[-1]
    lon_count = tr.shape[0]
    shape = (8, LANES)
    sub = lax.broadcasted_iota(jnp.int32, (8, columns), 0)
    upper = sub >= 4
    lane = lax.broadcasted_iota(jnp.int32, shape, 1)
    s0 = jnp.broadcast_to(shift[...], shape)
    s1 = s0 + 1
    here = jnp.broadcast_to(frac[...], shape)
    open_s8 = jnp.broadcast_to(open_s[...], (8, columns)) > 0
    open_n8 = jnp.broadcast_to(open_n[...], (8, columns)) > 0
    fold0, fold1 = (lane - s0) & (LANES - 1), (lane - s1) & (LANES - 1)
    own0, own1 = lane >= s0, lane >= s1

    def pair(ref_rows):
        a, b = ref_rows
        return jnp.where(upper, jnp.broadcast_to(b, (8, columns)), jnp.broadcast_to(a, (8, columns)))

    def tracer(t, carry):
        for seg in range(lon_count):
            x = jnp.concatenate([tr[seg, t, 0], tr[seg, t, 1]], axis=0)
            c = jnp.concatenate([cour[seg, 0], cour[seg, 1]], axis=0)
            lo = pair((south[seg, t, 0:1], south[seg, t, 1:2]))
            hi = pair((north_t[seg, t, 0:1], north_t[seg, t, 1:2]))
            ch = pair((north_c[seg, 0:1], north_c[seg, 1:2]))
            below = jnp.where((sub & 3) == 0, lo, pltpu.roll(x, 1, 0))
            flux = jnp.maximum(c, 0.0) * below + jnp.minimum(c, 0.0) * x
            flux = jnp.where(open_s8, flux, 0.0)
            edge = jnp.maximum(ch, 0.0) * x + jnp.minimum(ch, 0.0) * hi
            top = jnp.where((sub & 3) == 3, edge, pltpu.roll(flux, 7, 0))
            top = jnp.where(open_n8, top, 0.0)
            line[:, seg * columns : (seg + 1) * columns] = x + flux - top

        def gathered(p):
            tile = line[:, p * LANES : (p + 1) * LANES]
            return (
                jnp.take_along_axis(tile, fold0, axis=1),
                jnp.take_along_axis(tile, fold1, axis=1),
            )

        previous = gathered(PTS - 1)
        x = []
        for p in range(PTS):
            now = gathered(p)
            current = jnp.where(own0, now[0], previous[0])
            earlier = jnp.where(own1, now[1], previous[1])
            value = (1.0 - here) * current + here * earlier
            moved[t, :, p * LANES : (p + 1) * LANES] = value
            x.append(value)
            previous = now
        for r, (re, im) in enumerate(forward45(x)):
            tc, ts = twid[0, r : r + 1], twid[1, r : r + 1]
            row = pl.multiple_of((t * HALF + r) * 8, 8)
            if im is None:
                spec[pl.ds(row, 8), :LANES] = re * tc
                spec[pl.ds(row, 8), LANES:] = -(re * ts)
            else:
                spec[pl.ds(row, 8), :LANES] = re * tc + im * ts
                spec[pl.ds(row, 8), LANES:] = im * tc - re * ts
        return carry

    lax.fori_loop(0, tracer_count, tracer, 0)
    wave[...] = split_dot(spec[...], fwd_h[...], fwd_l[...])
    cut8 = jnp.broadcast_to(cut[...], shape)
    for r in range(HALF):
        weight = jnp.where(kabs[r : r + 1] <= cut8, scale[r : r + 1], 0.0)
        for t in range(tracer_count):
            row = (t * HALF + r) * 8
            wave[row : row + 8, :] = wave[row : row + 8, :] * weight
    spec[...] = split_dot(wave[...], inv_h[...], inv_l[...])

    damp8 = jnp.broadcast_to(damp[...], shape)
    cap8 = jnp.broadcast_to(cap[...], shape) > 0

    def back(t, carry):
        v = []
        for r in range(HALF):
            tc, ts = twid[0, r : r + 1], twid[1, r : r + 1]
            row = pl.multiple_of((t * HALF + r) * 8, 8)
            re, im = spec[pl.ds(row, 8), :LANES], spec[pl.ds(row, 8), LANES:]
            v.append((re * tc - im * ts, re * ts + im * tc))
        for p, low in enumerate(inverse45(v)):
            cols = slice(p * LANES, (p + 1) * LANES)
            shifted = moved[t, :, cols]
            filtered = damp8 * shifted + (1.0 - damp8) * low
            line[:, cols] = jnp.where(cap8, filtered, shifted)
        for seg in range(lon_count):
            value = line[:, seg * columns : (seg + 1) * columns]
            out[seg, t, 0] = value[:4]
            out[seg, t, 1] = value[4:]
        return carry

    lax.fori_loop(0, tracer_count, back, 0)


def compute(*operands, lon_count, tracer_count, columns):
    vmem = pl.BlockSpec(memory_space=pltpu.VMEM)
    rows = tracer_count * HALF * 8
    lon_cells = columns * lon_count
    return pl.pallas_call(
        compute_kernel,
        out_shape=jax.ShapeDtypeStruct((lon_count, tracer_count, 2, 4, columns), jnp.float32),
        in_specs=[vmem] * len(operands),
        out_specs=vmem,
        scratch_shapes=[
            pltpu.VMEM((8, lon_cells), jnp.float32),
            pltpu.VMEM((tracer_count, 8, lon_cells), jnp.float32),
            pltpu.VMEM((rows, 2 * LANES), jnp.float32),
            pltpu.VMEM((rows, LANES), jnp.float32),
        ],
        compiler_params=pltpu.CompilerParams(vmem_limit_bytes=40 << 20),
    )(*operands)


def greet(devices):
    barrier = pltpu.get_barrier_semaphore()
    for device in devices:
        pl.semaphore_signal(barrier, inc=1, device_id=device, device_id_type=MESH)
    pl.semaphore_wait(barrier, len(devices))


def gather_kernel(
    lat_count, lon_count, tr, cour, tr_top, tr_low, cour_low,
    got_t, got_c, south, north_t, north_c, send, recv, local,
):
    lat = lax.axis_index("lat")
    lon = lax.axis_index("lon")
    up = lax.rem(lat + 1, lat_count)
    down = lax.rem(lat + lat_count - 1, lat_count)
    turns = [lax.rem(lon + j, lon_count) for j in range(lon_count)]
    group = [{"lat": lat, "lon": turns[j]} for j in range(1, lon_count)]
    above = [{"lat": up, "lon": d} for d in turns]
    under = [{"lat": down, "lon": d} for d in turns]
    greet(group + above + under)
    copies = []

    def push(src, dst, device):
        index = len(copies)
        copy = pltpu.make_async_remote_copy(
            src_ref=src, dst_ref=dst, send_sem=send.at[index], recv_sem=recv.at[index],
            device_id=device, device_id_type=MESH,
        )
        copy.start()
        copies.append(copy)

    for j in (2, 1, 3):
        levels = pl.ds(2 * turns[j], 2)
        push(tr.at[:, levels], got_t.at[lon], group[j - 1])
        push(cour.at[levels], got_c.at[lon], group[j - 1])
    for j in (2, 1, 3, 0):
        levels = pl.ds(2 * turns[j], 2)
        push(tr_top.at[turns[j]], south.at[lon], above[j])
        push(tr_low.at[turns[j]], north_t.at[lon], under[j])
        push(cour_low.at[turns[j]], north_c.at[lon], under[j])
    mine = pl.ds(2 * lon, 2)
    keep_t = pltpu.make_async_copy(tr.at[:, mine], got_t.at[lon], local.at[0])
    keep_c = pltpu.make_async_copy(cour.at[mine], got_c.at[lon], local.at[1])
    keep_t.start()
    keep_c.start()
    for copy in copies:
        copy.wait()
    keep_t.wait()
    keep_c.wait()


def gather(tracers, courant, lat_count, lon_count):
    tracer_count, level_count, row_count, columns = tracers.shape
    per = level_count // lon_count

    def by_owner(edge):
        edge = edge.reshape(edge.shape[:-2] + (lon_count, per, columns))
        return jnp.moveaxis(edge, -3, 0)

    operands = (
        tracers, courant, by_owner(tracers[:, :, row_count - 1]),
        by_owner(tracers[:, :, 0]), by_owner(courant[:, 0]),
    )
    shapes = [
        (lon_count, tracer_count, per, row_count, columns),
        (lon_count, per, row_count, columns),
        (lon_count, tracer_count, per, columns),
        (lon_count, tracer_count, per, columns),
        (lon_count, per, columns),
    ]
    any_space = pl.BlockSpec(memory_space=pl.ANY)
    count = 2 * (lon_count - 1) + 3 * lon_count
    return pl.pallas_call(
        functools.partial(gather_kernel, lat_count, lon_count),
        out_shape=[jax.ShapeDtypeStruct(s, jnp.float32) for s in shapes],
        in_specs=[any_space] * len(operands),
        out_specs=[any_space] * len(shapes),
        scratch_shapes=[
            pltpu.SemaphoreType.DMA((count,)),
            pltpu.SemaphoreType.DMA((count,)),
            pltpu.SemaphoreType.DMA((2,)),
        ],
        compiler_params=pltpu.CompilerParams(collective_id=0, has_side_effects=True),
    )(*operands)


def return_kernel(lon_count, parts, out, send, recv, local):
    lon = lax.axis_index("lon")
    turns = [lax.rem(lon + j, lon_count) for j in range(lon_count)]
    greet([{"lon": d} for d in turns[1:]])
    mine = pl.ds(2 * lon, 2)
    copies = []
    for j in (2, 1, 3):
        copy = pltpu.make_async_remote_copy(
            src_ref=parts.at[turns[j]], dst_ref=out.at[:, mine],
            send_sem=send.at[j - 1], recv_sem=recv.at[j - 1],
            device_id={"lon": turns[j]}, device_id_type=MESH,
        )
        copy.start()
        copies.append(copy)
    keep = pltpu.make_async_copy(parts.at[lon], out.at[:, mine], local.at[0])
    keep.start()
    for copy in copies:
        copy.wait()
    keep.wait()


def send_back(parts, lon_count):
    _, tracer_count, per, row_count, columns = parts.shape
    any_space = pl.BlockSpec(memory_space=pl.ANY)
    return pl.pallas_call(
        functools.partial(return_kernel, lon_count),
        out_shape=jax.ShapeDtypeStruct((tracer_count, per * lon_count, row_count, columns), jnp.float32),
        in_specs=[any_space],
        out_specs=any_space,
        scratch_shapes=[
            pltpu.SemaphoreType.DMA((lon_count - 1,)),
            pltpu.SemaphoreType.DMA((lon_count - 1,)),
            pltpu.SemaphoreType.DMA((1,)),
        ],
        compiler_params=pltpu.CompilerParams(collective_id=1, has_side_effects=True),
    )(parts)


def body(tracers, merid_courant, zonal_shift, zonal_fraction, cutoff, damping):
    tracer_count, level_count, row_count, column_count = tracers.shape
    lat_count = lax.axis_size("lat")
    lat_index = lax.axis_index("lat")
    lon_count = lax.axis_size("lon")
    lon_index = lax.axis_index("lon")
    per = level_count // lon_count
    twid, kabs, scale, fwd, inv = tables(column_count * lon_count)
    pieces = gather(tracers, merid_courant, lat_count, lon_count)

    def own(levels):
        mine = lax.dynamic_slice_in_dim(levels, lon_index * per, per, axis=0)
        return mine.reshape(per * row_count, 1)

    def rows_of(values):
        mine = lax.dynamic_slice_in_dim(values, lat_index * row_count, row_count)
        return jnp.tile(mine, per).reshape(per * row_count, 1)

    row = jnp.tile(jnp.arange(row_count, dtype=jnp.int32), per).reshape(-1, 1)
    face = lat_index * row_count + row
    open_s = (face > 0).astype(jnp.int32)
    open_n = (face + 1 < lat_count * row_count).astype(jnp.int32)
    quarter = lat_count // 4
    is_cap = (lat_index < quarter) | (lat_index >= lat_count - quarter)
    cap = jnp.full((per * row_count, 1), is_cap, jnp.int32)
    parts = compute(
        *pieces, own(zonal_shift), own(zonal_fraction), rows_of(cutoff), rows_of(damping),
        open_s, open_n, cap, jnp.asarray(twid), jnp.asarray(kabs), jnp.asarray(scale),
        *halves(fwd), *halves(inv),
        lon_count=lon_count, tracer_count=tracer_count, columns=column_count,
    )
    return send_back(parts, lon_count)


def solution(mesh):
    placed = (
        P(None, None, "lat", "lon"),
        P(None, "lat", "lon"),
        P(None, "lat"),
        P(None, "lat"),
        P(),
        P(),
    )
    return jax.shard_map(
        body, mesh=mesh, in_specs=placed, out_specs=P(None, None, "lat", "lon"), check_vma=False
    )
```

time: 144 us -> 57.2 us (0.40)
  waiting for transfers between devices: 53.7 us -> 0 us
  Pallas kernels: 0 us -> 41.4 us
  other arithmetic: 32.3 us -> 0.01 us
  matrix products: 28.4 us -> 0 us
  between operations: 13.7 us -> 0.17 us
  starting transfers between devices: 10.3 us -> 0 us
  local copies, waits for them, and re-layouts: 5.68 us -> 15.2 us
    psum x1 -> x0, waiting for transfers between devices: 52.3 us -> none  [body(): coeffs = lax.psum(coeffs, 'lon')]
    pallas_call x0 -> x3, Pallas kernels: none -> 41.4 us  [the longest x1 25.2 us: gather(): pl.pallas_call(functools.partial(gather_kernel, lat_count, lon_count), ou...]
    dot_general x2 -> x0, matrix products: 28.4 us -> none  [the longest x1 16.6 us: body(): jnp.dot(coeffs.reshape(-1, 2 * MODES), basis_table.T, precision=lax.Preci...]
    cos x1 -> x0, other arithmetic: 27.2 us -> none  [make_basis(): return jnp.concatenate([jnp.cos(angles), jnp.sin(angles)], axis=1)]
    ppermute x3 -> x0, starting transfers between devices: 10.3 us -> none  [the longest x2 7.57 us: passed_along(): return lax.ppermute(block, axis, route)]
    unnamed x12 -> x35, local copies, waits for them, and re-layouts: 2.4 us -> 9.59 us
    slice x3 -> x4, local copies, waits for them, and re-layouts: 0.12 us -> 3.11 us  [the longest x2 1.92 us: gather(): tracers[:, :, 0]]
    select_n x9 -> x0, other arithmetic: 2.43 us -> none  [the longest x7 2.12 us: body(): moved = jnp.where(selected, pushed, moved)]
  transfers between devices with their start and end apart: 4 -> 0, of which waited for: 2 -> 0; matrix products, arithmetic and copies ran while one was open for 20% -> 0% of each run, Pallas kernels for 0% -> 0%
where the time goes in v1:
time: 57.2 us; the launch traced here: 56.8 us
  Pallas kernels  41.4 us (72%)
  local copies, waits for them, and re-layouts  15.2 us (27%)
    pallas_call x1, Pallas kernels, gather(): pl.pallas_call(functools.partial(gather_kernel, lat_count, lon_count), ou...  25.2 us
    pallas_call x1, Pallas kernels, send_back(): pl.pallas_call(functools.partial(return_kernel, lon_count), out_shape=jax...  12.1 us
    unnamed x35, local copies, waits for them, and re-layouts  9.59 us
    pallas_call x1, Pallas kernels, compute(): pl.pallas_call(compute_kernel, out_shape=jax.ShapeDtypeStruct((lon_count,...  4.11 us
    slice x2, local copies, waits for them, and re-layouts, gather(): tracers[:, :, 0]  1.92 us

profile of v1, /device:TPU:1, one launch (start us, length us, event | category | flops | bytes accessed | tf_op | source)
XLA Modules:
  0.0 56.8 jit_solution(6216522608036528869)
XLA Ops:
  0.0 0.0 copy-start
  0.0 0.0 copy-start.15
  0.0 0.7 %copy-done.15 = s32[256]{0:T(256)S(1)} copy-done((s32[256]{0:T(256)S(1)}, s32[256]{0:T(256)}, u32[]{:S(2)}) %copy-start.15) | copy-done | bytes 1048
  0.7 0.0 copy-start.16
  0.7 0.1 dynamic_slice.14
  0.8 0.6 %copy-done.16 = f32[256]{0:T(256)S(1)} copy-done((f32[256]{0:T(256)S(1)}, f32[256]{0:T(256)}, u32[]{:S(2)}) %copy-start.16) | copy-done | bytes 1048
  1.4 0.1 dynamic_slice.15
  1.5 0.0 copy-done
  1.5 0.1 constant_dynamic-slice_fusion.1
  1.6 0.0 copy-start.14
  1.6 0.1 copy.24
  1.6 0.6 %copy-done.14 = f32[8,4]{0,1:T(4,128)S(1)} copy-done((f32[8,4]{0,1:T(4,128)S(1)}, f32[8,4]{0,1:T(4,128)}, u32[]{:S(2)}) %copy-start.14) | copy-done | bytes 152
  2.2 0.1 constant_dynamic-slice_fusion
  2.3 0.1 copy.25
  2.4 0.1 reshape.61.frac
  2.5 0.1 reshape.60.shift
  2.6 0.1 reshape.63.open_n
  2.6 0.1 reshape_tile.9.cut
  2.7 0.1 reshape_tile.10.damp
  2.8 0.1 reshape.62.open_s
  2.9 1.1 %slice_reduce_fusion = f32[8,1440]{1,0:T(8,128)S(1)} fusion(f32[8,4,1440]{2,1,0:T(4,128)} %cour.1), kind=kLoop, calls=%fused_computation.2 | loop fusion | bytes 92160 | tf_op jit(solution)/shard_map/slice | solution.py:343
  3.9 0.6 %reshape_squeeze.11.cour_low = f32[4,2,1440]{2,1,0:T(2,128)} reshape(f32[8,1440]{1,0:T(8,128)S(1)} %slice_reduce_fusion) | data formatting | bytes 92160 | tf_op jit(solution)/shard_map/reshape;squeeze | solution.py:338
  4.6 1.8 %fusion = (f32[4,8,1,1440]{3,2,1,0:T(1,128)S(1)}, f32[4,8,1,1440]{3,2,1,0:T(1,128)S(1)}) fusion(f32[4,8,4,1440]{3,2,1,0:T(4,128)} %tr.1), kind=kLoop, calls=%fused_computation.8 | loop fusion | bytes 737280 | tf_op jit(solution)/shard_map/slice | solution.py:343
  6.4 0.1 copy.22
  6.5 0.1 copy.20
  6.6 1.0 %copy_bitcast_fusion = (f32[4,4,2,1440]{3,2,1,0:T(2,128)}, f32[4,4,2,1440]{3,2,1,0:T(2,128)}) fusion(f32[4,4,2,1440]{3,0,2,1:T(4,128)S(1)} %bitcast.6, f32[4,4,2,1440]{3,0,2,1:T(4,128)S(1)} %bitcast.7), kind=kLoop, calls=%fused_computation | loop fusion | bytes 737280 | tf_op jit(solution)/shard_map/transpose | solution.py:339
  7.6 0.0 copy-start.6
  7.6 0.0 copy-start.7
  7.6 0.0 copy-start.8
  7.6 0.0 copy-start.9
  7.6 0.0 copy-start.11
  7.6 0.0 copy-start.12
  7.6 0.0 copy-start.13
  7.6 25.2 %shard_map.109 = (f32[4,4,2,4,1440]{4,3,2,1,0:T(4,128)}, f32[4,2,4,1440]{3,2,1,0:T(4,128)}, f32[4,4,2,1440]{3,2,1,0:T(2,128)}, f32[4,4,2,1440]{3,2,1,0:T(2,128)}, f32[4,2,1440]{2,1,0:T(2,128)}) custom-call(f32[4,8,4,1440]{3,2,1,0:T(4,128)} %tr.1, f32[8,4,1440]{2,1,0:T(4,128)} %cour.1, f32[4,4,2,1440]{3,2,1,0:T(2,128)} %get-tuple-element.18.tr_top, ...), custom_call_target="tpu_custom_call" | custom-call | tf_op jit(solution)/shard_map/pallas_call | solution.py:354
  32.9 0.0 copy-done.6
  32.9 0.0 copy-done.7
  32.9 0.0 copy-done.8
  32.9 0.0 copy-done.9
  32.9 0.0 copy-done.11
  32.9 0.0 copy-done.12
  32.9 0.0 copy-done.13
  32.9 0.0 copy-start.2
  32.9 1.1 %copy-done.2 = f32[4,4,2,4,1440]{4,3,2,1,0:T(4,128)S(1)} copy-done((f32[4,4,2,4,1440]{4,3,2,1,0:T(4,128)S(1)}, f32[4,4,2,4,1440]{4,3,2,1,0:T(4,128)}, u32[]{:S(2)}) %copy-start.2) | copy-done | bytes 737304
  34.1 0.0 copy-start.3
  34.1 0.9 %copy-done.3 = f32[4,2,4,1440]{3,2,1,0:T(4,128)S(1)} copy-done((f32[4,2,4,1440]{3,2,1,0:T(4,128)S(1)}, f32[4,2,4,1440]{3,2,1,0:T(4,128)}, u32[]{:S(2)}) %copy-start.3) | copy-done | bytes 184344
  35.0 0.0 copy-start.4
  35.0 0.9 %copy-done.4 = f32[4,4,2,1440]{3,2,1,0:T(2,128)S(1)} copy-done((f32[4,4,2,1440]{3,2,1,0:T(2,128)S(1)}, f32[4,4,2,1440]{3,2,1,0:T(2,128)}, u32[]{:S(2)}) %copy-start.4) | copy-done | bytes 184344
  35.9 0.0 copy-start.5
  35.9 0.9 %copy-done.5 = f32[4,4,2,1440]{3,2,1,0:T(2,128)S(1)} copy-done((f32[4,4,2,1440]{3,2,1,0:T(2,128)S(1)}, f32[4,4,2,1440]{3,2,1,0:T(2,128)}, u32[]{:S(2)}) %copy-start.5) | copy-done | bytes 184344
  36.9 0.0 copy-start.10
  36.9 0.8 %copy-done.10 = f32[4,2,1440]{2,1,0:T(2,128)S(1)} copy-done((f32[4,2,1440]{2,1,0:T(2,128)S(1)}, f32[4,2,1440]{2,1,0:T(2,128)}, u32[]{:S(2)}) %copy-start.10) | copy-done | bytes 46104
  37.7 4.1 %shard_map.110.parts = f32[4,4,2,4,1440]{4,3,2,1,0:T(4,128)S(1)} custom-call(f32[4,4,2,4,1440]{4,3,2,1,0:T(4,128)S(1)} %copy-done.2, f32[4,2,4,1440]{3,2,1,0:T(4,128)S(1)} %copy-done.3, f32[4,4,2,1440]{3,2,1,0:T(2,128)S(1)} %copy-done.4, f32[4,4,2,1440]{3,2,1,0:T(2,128)S(1)} %copy-done.5, f32[4,2,1440]{2,1,0:T(2,128)S(1)} %copy-done.10, ...), custom_call_target="tpu_custom_call" | custom-call | tf_op jit(solution)/shard_map/pallas_call | solution.py:267
  41.8 0.0 copy-start.1
  41.8 0.9 %copy-done.1 = f32[4,4,2,4,1440]{4,3,2,1,0:T(4,128)} copy-done((f32[4,4,2,4,1440]{4,3,2,1,0:T(4,128)}, f32[4,4,2,4,1440]{4,3,2,1,0:T(4,128)S(1)}, u32[]{:S(2)}) %copy-start.1) | copy-done | bytes 737304
  42.7 12.1 %shard_map.111 = f32[4,8,4,1440]{3,2,1,0:T(4,128)} custom-call(f32[4,4,2,4,1440]{4,3,2,1,0:T(4,128)} %copy-done.1), custom_call_target="tpu_custom_call" | custom-call | tf_op jit(solution)/shard_map/pallas_call | solution.py:392
  54.7 2.1 %copy.36 = f32[4,8,4,1440]{3,2,1,0:T(4,128)} copy(f32[4,8,4,1440]{3,2,1,0:T(4,128)} %shard_map.111) | data formatting | bytes 1474560
  (4 shorter events, 0.0 us)
Async XLA Ops:
  0.0 1.5 %copy-start = (s32[8,4]{0,1:T(4,128)S(1)}, s32[8,4]{0,1:T(4,128)}, u32[]{:S(2)}) copy-start(s32[8,4]{0,1:T(4,128)} %param.13) | copy-start | bytes 388
  0.0 0.7 %copy-start.15 = (s32[256]{0:T(256)S(1)}, s32[256]{0:T(256)}, u32[]{:S(2)}) copy-start(s32[256]{0:T(256)} %param.15) | copy-start | bytes 3076
  0.7 0.7 %copy-start.16 = (f32[256]{0:T(256)S(1)}, f32[256]{0:T(256)}, u32[]{:S(2)}) copy-start(f32[256]{0:T(256)} %param.16) | copy-start | bytes 3076
  1.6 0.7 %copy-start.14 = (f32[8,4]{0,1:T(4,128)S(1)}, f32[8,4]{0,1:T(4,128)}, u32[]{:S(2)}) copy-start(f32[8,4]{0,1:T(4,128)} %param.14) | copy-start | bytes 388
  7.6 25.3 %copy-start.6 = (bf16[128,256]{1,0:T(8,128)(2,1)S(1)}, bf16[128,256]{1,0:T(8,128)(2,1)}, u32[]{:S(2)}) copy-start(bf16[128,256]{1,0:T(8,128)(2,1)} %constant.53.inv_l) | copy-start | bytes 196612
  7.6 25.3 %copy-start.7 = (bf16[128,256]{1,0:T(8,128)(2,1)S(1)}, bf16[128,256]{1,0:T(8,128)(2,1)}, u32[]{:S(2)}) copy-start(bf16[128,256]{1,0:T(8,128)(2,1)} %constant.50.inv_h) | copy-start | bytes 196612
  7.6 25.3 %copy-start.8 = (bf16[256,128]{1,0:T(8,128)(2,1)S(1)}, bf16[256,128]{1,0:T(8,128)(2,1)}, u32[]{:S(2)}) copy-start(bf16[256,128]{1,0:T(8,128)(2,1)} %constant.49.fwd_l) | copy-start | bytes 196612
  7.6 25.3 %copy-start.9 = (bf16[256,128]{1,0:T(8,128)(2,1)S(1)}, bf16[256,128]{1,0:T(8,128)(2,1)}, u32[]{:S(2)}) copy-start(bf16[256,128]{1,0:T(8,128)(2,1)} %constant.46.fwd_h) | copy-start | bytes 196612
  7.6 25.3 %copy-start.11 = (f32[2,23,128]{2,1,0:T(8,128)S(1)}, f32[2,23,128]{2,1,0:T(8,128)}, u32[]{:S(2)}) copy-start(f32[2,23,128]{2,1,0:T(8,128)} %constant.37.clone.twid) | copy-start | bytes 70660
  7.6 25.3 %copy-start.12 = (f32[23,128]{1,0:T(8,128)S(1)}, f32[23,128]{1,0:T(8,128)}, u32[]{:S(2)}) copy-start(f32[23,128]{1,0:T(8,128)} %constant.39.clone.scale) | copy-start | bytes 35332
  7.6 25.3 %copy-start.13 = (s32[23,128]{1,0:T(8,128)S(1)}, s32[23,128]{1,0:T(8,128)}, u32[]{:S(2)}) copy-start(s32[23,128]{1,0:T(8,128)} %constant.38.clone.kabs) | copy-start | bytes 35332
  32.9 1.1 %copy-start.2 = (f32[4,4,2,4,1440]{4,3,2,1,0:T(4,128)S(1)}, f32[4,4,2,4,1440]{4,3,2,1,0:T(4,128)}, u32[]{:S(2)}) copy-start(f32[4,4,2,4,1440]{4,3,2,1,0:T(4,128)} %get-tuple-element.10.tr) | copy-start | bytes 2211844
  34.1 0.9 %copy-start.3 = (f32[4,2,4,1440]{3,2,1,0:T(4,128)S(1)}, f32[4,2,4,1440]{3,2,1,0:T(4,128)}, u32[]{:S(2)}) copy-start(f32[4,2,4,1440]{3,2,1,0:T(4,128)} %get-tuple-element.11.cour) | copy-start | bytes 552964
  35.0 0.9 %copy-start.4 = (f32[4,4,2,1440]{3,2,1,0:T(2,128)S(1)}, f32[4,4,2,1440]{3,2,1,0:T(2,128)}, u32[]{:S(2)}) copy-start(f32[4,4,2,1440]{3,2,1,0:T(2,128)} %get-tuple-element.12.south) | copy-start | bytes 552964
  35.9 0.9 %copy-start.5 = (f32[4,4,2,1440]{3,2,1,0:T(2,128)S(1)}, f32[4,4,2,1440]{3,2,1,0:T(2,128)}, u32[]{:S(2)}) copy-start(f32[4,4,2,1440]{3,2,1,0:T(2,128)} %get-tuple-element.13.north_t) | copy-start | bytes 552964
  36.9 0.8 %copy-start.10 = (f32[4,2,1440]{2,1,0:T(2,128)S(1)}, f32[4,2,1440]{2,1,0:T(2,128)}, u32[]{:S(2)}) copy-start(f32[4,2,1440]{2,1,0:T(2,128)} %get-tuple-element.14.north_c) | copy-start | bytes 138244
  41.8 0.9 %copy-start.1 = (f32[4,4,2,4,1440]{4,3,2,1,0:T(4,128)}, f32[4,4,2,4,1440]{4,3,2,1,0:T(4,128)S(1)}, u32[]{:S(2)}) copy-start(f32[4,4,2,4,1440]{4,3,2,1,0:T(4,128)S(1)} %shard_map.110.parts) | copy-start | bytes 2211844

commit v2 on v1

v2 whole, which is shorter than its diff:
```python
import functools
import math

import jax
import jax.numpy as jnp
import numpy as np
from jax import lax
from jax.experimental import pallas as pl
from jax.experimental.pallas import tpu as pltpu
from jax.sharding import PartitionSpec as P

MODES = 1024
LANES = 128
PTS = 45
HALF = 23
SPAN = 23
MESH = pl.DeviceIdType.MESH


def residues():
    found = []
    for k5 in range(3):
        for k9 in range(5 if k5 == 0 else 9):
            kk = next(k for k in range(PTS) if k % 5 == k5 and k % 9 == k9)
            found.append(kk if kk <= PTS // 2 else kk - PTS)
    return found


def tables(lon_cells):
    res = np.array(residues(), np.int64)
    lane = np.arange(LANES, dtype=np.int64)
    ang = (res[:, None] * lane[None, :] % lon_cells) * (2 * math.pi / lon_cells)
    twid = np.stack([np.cos(ang), np.sin(ang)]).astype(np.float32)
    half = LANES // 2
    k2 = np.zeros(LANES, np.int64)
    valid = np.zeros(LANES, bool)
    for part in range(2):
        k2[part * half : part * half + 2 * SPAN + 1] = np.arange(-SPAN, SPAN + 1)
        valid[part * half : part * half + 2 * SPAN + 1] = True
    mode = res[:, None] + PTS * k2[None, :]
    kabs = np.abs(mode)
    keep = valid[None, :] & (kabs < MODES) & ~((res[:, None] == 0) & (mode < 0))
    kabs = np.where(keep, kabs, 1 << 20).astype(np.int32)
    scale = np.where(mode == 0, 1.0, 2.0) / lon_cells
    scale = np.where(keep, scale, 0.0).astype(np.float32)
    ang2 = (k2[None, :] * lane[:, None] % LANES) * (2 * math.pi / LANES)
    c2 = np.cos(ang2) * valid[None, :]
    s2 = np.sin(ang2) * valid[None, :]
    first = np.arange(LANES) < half
    fwd = np.concatenate(
        [np.where(first, c2, -s2), np.where(first, s2, c2)], axis=0
    )
    inv = np.concatenate(
        [np.where(first, c2, -s2), np.where(first, s2, c2)], axis=0
    ).T
    return twid, kabs, scale, fwd.astype(np.float32), inv.astype(np.float32)


def halves(table):
    high = jnp.asarray(table).astype(jnp.bfloat16)
    low = (jnp.asarray(table) - high.astype(jnp.float32)).astype(jnp.bfloat16)
    return high, low


def split_dot(value, high, low):
    vh = value.astype(jnp.bfloat16)
    vl = (value - vh.astype(jnp.float32)).astype(jnp.bfloat16)
    dot = functools.partial(jnp.dot, preferred_element_type=jnp.float32)
    return dot(vh, high) + (dot(vl, high) + dot(vh, low))


def cs(count, turn):
    return math.cos(2 * math.pi * turn / count), math.sin(2 * math.pi * turn / count)


def real5(x):
    e1, o1, e2, o2 = x[1] + x[4], x[1] - x[4], x[2] + x[3], x[2] - x[3]
    c1, s1 = cs(5, 1)
    c2, s2 = cs(5, 2)
    return (
        x[0] + (e1 + e2),
        (x[0] + (c1 * e1 + c2 * e2), -(s1 * o1 + s2 * o2)),
        (x[0] + (c2 * e1 + c1 * e2), s1 * o2 - s2 * o1),
    )


def total(terms):
    while len(terms) > 1:
        terms = [sum(terms[i : i + 2][1:], terms[i]) for i in range(0, len(terms), 2)]
    return terms[0]


def real9(x):
    e = [x[j] + x[9 - j] for j in range(1, 5)]
    o = [x[j] - x[9 - j] for j in range(1, 5)]
    out = [(total([x[0]] + e), None)]
    for k in range(1, 5):
        re = total([x[0]] + [cs(9, j * k)[0] * e[j - 1] for j in range(1, 5)])
        im = total([-cs(9, j * k)[1] * o[j - 1] for j in range(1, 5)])
        out.append((re, im))
    return out


def complex9(re, im, sign):
    er = [re[j] + re[9 - j] for j in range(1, 5)]
    ei = [im[j] + im[9 - j] for j in range(1, 5)]
    dr = [re[j] - re[9 - j] for j in range(1, 5)]
    di = [im[j] - im[9 - j] for j in range(1, 5)]
    out = [None] * 9
    out[0] = (total([re[0]] + er), total([im[0]] + ei))
    for k in range(1, 5):
        c = [cs(9, j * k)[0] for j in range(1, 5)]
        s = [sign * cs(9, j * k)[1] for j in range(1, 5)]
        pr = total([re[0]] + [c[j] * er[j] for j in range(4)])
        pi = total([im[0]] + [c[j] * ei[j] for j in range(4)])
        qr = total([s[j] * di[j] for j in range(4)])
        qi = total([s[j] * dr[j] for j in range(4)])
        out[k] = (pr - qr, pi + qi)
        out[9 - k] = (pr + qr, pi - qi)
    return out


def forward45(x):
    zero, one, two = [], [], []
    for p9 in range(9):
        a0, a1, a2 = real5([x[(9 * p5 + 5 * p9) % PTS] for p5 in range(5)])
        zero.append(a0)
        one.append(a1)
        two.append(a2)
    out = real9(zero)
    for part in (one, two):
        out += complex9([a[0] for a in part], [a[1] for a in part], -1.0)
    return out


def inverse45(v):
    zero, one, two = v[:5], v[5:14], v[14:]
    b0 = [None] * 9
    b0[0] = total([z[0] for z in zero])
    for p in range(1, 5):
        pr = total([zero[0][0]] + [cs(9, p * k)[0] * zero[k][0] for k in range(1, 5)])
        qr = total([cs(9, p * k)[1] * zero[k][1] for k in range(1, 5)])
        b0[p] = pr - qr
        b0[9 - p] = pr + qr
    b1 = complex9([a[0] for a in one], [a[1] for a in one], 1.0)
    b2 = complex9([a[0] for a in two], [a[1] for a in two], 1.0)
    c1, s1 = cs(5, 1)
    c2, s2 = cs(5, 2)
    out = [None] * PTS
    for p9 in range(9):
        (r1, i1), (r2, i2), base = b1[p9], b2[p9], b0[p9]
        ca = base + (c1 * r1 + c2 * r2)
        sa = s1 * i1 + s2 * i2
        cb = base + (c2 * r1 + c1 * r2)
        sb = s2 * i1 - s1 * i2
        vals = [base + (r1 + r2), ca - sa, cb - sb, cb + sb, ca + sa]
        for p5 in range(5):
            out[(9 * p5 + 5 * p9) % PTS] = vals[p5]
    return out


def fused_kernel(
    lat_count, lon_count,
    tr, cour, zs_in, zf_in, cut_in, damp_in,
    twid_in, kabs_in, scale_in, fwd_h_in, fwd_l_in, inv_h_in, inv_l_in,
    out,
    got_t, got_c, halo_t, halo_c, parts,
    zs, zf, cut, damp, twid, kabs, scale, fwd_h, fwd_l, inv_h, inv_l,
    line, moved, spec, wave,
    t_send, t_recv, c_send, c_recv, h_send, h_recv, hc_send, hc_recv, b_send, b_recv, b_local, local,
):
    tracer_count, _, row_count, columns = tr.shape
    lat = lax.axis_index("lat")
    lon = lax.axis_index("lon")
    up = lax.rem(lat + 1, lat_count)
    down = lax.rem(lat + lat_count - 1, lat_count)
    flip = 2 * lax.rem(lat, 2)
    peers = [lon + 1 - 2 * lax.rem(lon, 2), lax.rem(lon + 2, lon_count), lon_count - 1 - lon]
    levels = [pl.ds(2 * lax.rem(peer + flip, lon_count), 2) for peer in peers]
    mine = pl.ds(2 * lax.rem(lon + flip, lon_count), 2)
    across = peers[1]
    near = 2 * (lon // 2)
    pairs = [near, 2 - near]

    staged = [
        (tr.at[:, mine], got_t.at[lon]), (cour.at[mine], got_c.at[lon]),
        (zs_in, zs), (zf_in, zf), (cut_in, cut), (damp_in, damp),
        (twid_in, twid), (kabs_in, kabs), (scale_in, scale),
        (fwd_h_in, fwd_h), (fwd_l_in, fwd_l), (inv_h_in, inv_h), (inv_l_in, inv_l),
    ]
    staged = [
        pltpu.make_async_copy(a, b, local.at[i]) for i, (a, b) in enumerate(staged)
    ]
    for copy in staged:
        copy.start()

    def remote(src, dst, send, recv, device):
        return pltpu.make_async_remote_copy(
            src_ref=src, dst_ref=dst, send_sem=send, recv_sem=recv,
            device_id=device, device_id_type=MESH,
        )

    def cells(t, m):
        return remote(
            tr.at[t, levels[m]], got_t.at[lon, t], t_send.at[t, m], t_recv.at[t, m],
            {"lat": lat, "lon": peers[m]},
        )

    def speeds(m):
        return remote(
            cour.at[levels[m]], got_c.at[lon], c_send.at[m], c_recv.at[m],
            {"lat": lat, "lon": peers[m]},
        )

    def rims(t, k):
        both = pl.ds(pairs[k], 2)
        north = remote(
            got_t.at[both, t, :, pl.ds(row_count - 1, 1)],
            halo_t.at[both, t, :, pl.ds(row_count - 1, 1)],
            h_send.at[t, k], h_recv.at[t, k], {"lat": up, "lon": across},
        )
        south = remote(
            got_t.at[both, t, :, pl.ds(0, 1)],
            halo_t.at[both, t, :, pl.ds(0, 1)],
            h_send.at[t, k + 2], h_recv.at[t, k + 2], {"lat": down, "lon": across},
        )
        return north, south

    def rim_speed(k):
        both = pl.ds(pairs[k], 2)
        return remote(
            got_c.at[both, :, pl.ds(0, 1)], halo_c.at[both, :, pl.ds(0, 1)],
            hc_send.at[k], hc_recv.at[k], {"lat": down, "lon": across},
        )

    def reply(t, m):
        return remote(
            parts.at[peers[m], t], out.at[t, mine], b_send.at[t, m], b_recv.at[t, m],
            {"lat": lat, "lon": peers[m]},
        )

    def keep(t):
        return pltpu.make_async_copy(parts.at[lon, t], out.at[t, mine], b_local.at[t])

    barrier = pltpu.get_barrier_semaphore()
    friends = [{"lat": lat, "lon": peer} for peer in peers]
    friends += [{"lat": up, "lon": across}, {"lat": down, "lon": across}]
    for friend in friends:
        pl.semaphore_signal(barrier, inc=1, device_id=friend, device_id_type=MESH)
    pl.semaphore_wait(barrier, len(friends))

    for m in (1, 2, 0):
        speeds(m).start()
    for t in range(tracer_count):
        for m in (1, 2, 0):
            cells(t, m).start()
    for copy in staged:
        copy.wait()

    def relay(t):
        cells(t, 0).wait_recv()
        for copy in rims(t, 0):
            copy.start()
        cells(t, 1).wait_recv()
        cells(t, 2).wait_recv()
        for copy in rims(t, 1):
            copy.start()

    speeds(0).wait_recv()
    rim_speed(0).start()
    speeds(1).wait_recv()
    speeds(2).wait_recv()
    rim_speed(1).start()
    relay(0)

    shape = (8, LANES)
    sub = lax.broadcasted_iota(jnp.int32, (8, columns), 0)
    sub1 = lax.broadcasted_iota(jnp.int32, shape, 0)
    lane = lax.broadcasted_iota(jnp.int32, shape, 1)

    def own_levels(ref):
        rows = ref[mine].astype(jnp.float32)
        wide = jnp.concatenate(
            [jnp.broadcast_to(rows[i : i + 1], (4, row_count)) for i in range(2)], axis=0
        )
        a = lax.broadcasted_iota(jnp.int32, wide.shape, 0)
        b = lax.broadcasted_iota(jnp.int32, wide.shape, 1)
        value = jnp.sum(jnp.where(b == (a & 3), wide, 0.0), axis=1, keepdims=True)
        return jnp.broadcast_to(value, shape)

    def own_rows(ref):
        rows = ref[pl.ds(lat * row_count // LANES, 1)].astype(jnp.float32)
        wide = jnp.broadcast_to(rows, shape)
        at = lax.rem(lat * row_count, LANES) + (sub1 & 3)
        value = jnp.sum(jnp.where(lane == at, wide, 0.0), axis=1, keepdims=True)
        return jnp.broadcast_to(value, shape)

    s0 = own_levels(zs).astype(jnp.int32)
    s1 = s0 + 1
    here = own_levels(zf)
    cut8 = own_rows(cut).astype(jnp.int32)
    damp8 = own_rows(damp)
    face = lat * row_count + (sub & 3)
    open_s8 = face > 0
    open_n8 = face + 1 < lat_count * row_count
    band = lat + 0 * lane
    quarter = lat_count // 4
    cap8 = (band < quarter) | (band >= lat_count - quarter)
    fold0, fold1 = (lane - s0) & (LANES - 1), (lane - s1) & (LANES - 1)
    own0, own1 = lane >= s0, lane >= s1

    def stacked(ref, *at):
        return jnp.concatenate([ref[(*at, 0)], ref[(*at, 1)]], axis=0)

    def tracer(t, carry):
        @pl.when(t < tracer_count - 1)
        def _():
            relay(t + 1)

        for k in range(2):
            for copy in rims(t, k):
                copy.wait_recv()
        for seg in range(lon_count):
            x = stacked(got_t, seg, t)
            c = stacked(got_c, seg)
            rim = stacked(halo_t, seg, t)
            rim_c = stacked(halo_c, seg)
            below = jnp.where((sub & 3) == 0, pltpu.roll(rim, 5, 0), pltpu.roll(x, 1, 0))
            flux = jnp.maximum(c, 0.0) * below + jnp.minimum(c, 0.0) * x
            flux = jnp.where(open_s8, flux, 0.0)
            hi, ch = pltpu.roll(rim, 3, 0), pltpu.roll(rim_c, 3, 0)
            edge = jnp.maximum(ch, 0.0) * x + jnp.minimum(ch, 0.0) * hi
            top = jnp.where((sub & 3) == 3, edge, pltpu.roll(flux, 7, 0))
            top = jnp.where(open_n8, top, 0.0)
            line[:, seg * columns : (seg + 1) * columns] = x + flux - top

        def gathered(p):
            tile = line[:, p * LANES : (p + 1) * LANES]
            return (
                jnp.take_along_axis(tile, fold0, axis=1),
                jnp.take_along_axis(tile, fold1, axis=1),
            )

        previous = gathered(PTS - 1)
        x = []
        for p in range(PTS):
            now = gathered(p)
            current = jnp.where(own0, now[0], previous[0])
            earlier = jnp.where(own1, now[1], previous[1])
            value = (1.0 - here) * current + here * earlier
            moved[:, p * LANES : (p + 1) * LANES] = value
            x.append(value)
            previous = now
        for r, (re, im) in enumerate(forward45(x)):
            tc, ts = twid[0, r : r + 1], twid[1, r : r + 1]
            if im is None:
                spec[8 * r : 8 * r + 8, :LANES] = re * tc
                spec[8 * r : 8 * r + 8, LANES:] = -(re * ts)
            else:
                spec[8 * r : 8 * r + 8, :LANES] = re * tc + im * ts
                spec[8 * r : 8 * r + 8, LANES:] = im * tc - re * ts
        wave[...] = split_dot(spec[...], fwd_h[...], fwd_l[...])
        for r in range(HALF):
            weight = jnp.where(kabs[r : r + 1] <= cut8, scale[r : r + 1], 0.0)
            wave[8 * r : 8 * r + 8, :] = wave[8 * r : 8 * r + 8, :] * weight
        spec[...] = split_dot(wave[...], inv_h[...], inv_l[...])
        v = []
        for r in range(HALF):
            tc, ts = twid[0, r : r + 1], twid[1, r : r + 1]
            re, im = spec[8 * r : 8 * r + 8, :LANES], spec[8 * r : 8 * r + 8, LANES:]
            v.append((re * tc - im * ts, re * ts + im * tc))
        for p, low in enumerate(inverse45(v)):
            cols = slice(p * LANES, (p + 1) * LANES)
            shifted = moved[:, cols]
            filtered = damp8 * shifted + (1.0 - damp8) * low
            line[:, cols] = jnp.where(cap8, filtered, shifted)
        for seg in range(lon_count):
            value = line[:, seg * columns : (seg + 1) * columns]
            parts[seg, t, 0] = value[:4]
            parts[seg, t, 1] = value[4:]
        for m in (1, 2, 0):
            reply(t, m).start()
        keep(t).start()
        return carry

    for k in range(2):
        rim_speed(k).wait_recv()
    lax.fori_loop(0, tracer_count, tracer, 0)

    for m in range(3):
        speeds(m).wait_send()
    for k in range(2):
        rim_speed(k).wait_send()
    for t in range(tracer_count):
        for m in range(3):
            cells(t, m).wait_send()
        for k in range(2):
            for copy in rims(t, k):
                copy.wait_send()
        for m in range(3):
            reply(t, m).wait_send()
            back = reply(t, m)
            back.wait_recv()
        keep(t).wait()


def body(tracers, merid_courant, zonal_shift, zonal_fraction, cutoff, damping):
    tracer_count, level_count, row_count, columns = tracers.shape
    lat_count = lax.axis_size("lat")
    lon_count = lax.axis_size("lon")
    per = level_count // lon_count
    twid, kabs, scale, fwd, inv = tables(columns * lon_count)
    operands = (
        tracers, merid_courant, zonal_shift, zonal_fraction,
        cutoff.reshape(-1, LANES), damping.reshape(-1, LANES),
        jnp.asarray(twid), jnp.asarray(kabs), jnp.asarray(scale), *halves(fwd), *halves(inv),
    )
    any_space = pl.BlockSpec(memory_space=pl.ANY)
    tile = (per, row_count, columns)
    f32 = jnp.float32
    small = [pltpu.VMEM(a.shape, a.dtype) for a in operands[2:]]
    dma = pltpu.SemaphoreType.DMA
    return pl.pallas_call(
        functools.partial(fused_kernel, lat_count, lon_count),
        out_shape=jax.ShapeDtypeStruct(tracers.shape, f32),
        in_specs=[any_space] * len(operands),
        out_specs=any_space,
        scratch_shapes=[
            pltpu.VMEM((lon_count, tracer_count) + tile, f32),
            pltpu.VMEM((lon_count,) + tile, f32),
            pltpu.VMEM((lon_count, tracer_count) + tile, f32),
            pltpu.VMEM((lon_count,) + tile, f32),
            pltpu.VMEM((lon_count, tracer_count) + tile, f32),
            *small,
            pltpu.VMEM((8, columns * lon_count), f32),
            pltpu.VMEM((8, columns * lon_count), f32),
            pltpu.VMEM((HALF * 8, 2 * LANES), f32),
            pltpu.VMEM((HALF * 8, LANES), f32),
            dma((tracer_count, 3)), dma((tracer_count, 3)),
            dma((3,)), dma((3,)),
            dma((tracer_count, 4)), dma((tracer_count, 4)),
            dma((2,)), dma((2,)),
            dma((tracer_count, 3)), dma((tracer_count, 3)),
            dma((tracer_count,)),
            dma((len(operands),)),
        ],
        compiler_params=pltpu.CompilerParams(collective_id=0, has_side_effects=True),
    )(*operands)


def solution(mesh):
    placed = (
        P(None, None, "lat", "lon"),
        P(None, "lat", "lon"),
        P(None, "lat"),
        P(None, "lat"),
        P(),
        P(),
    )
    return jax.shard_map(
        body, mesh=mesh, in_specs=placed, out_specs=P(None, None, "lat", "lon"), check_vma=False
    )
```

time: 57.2 us -> 41.2 us (0.72)
  local copies, waits for them, and re-layouts: 15.2 us -> 4.12 us
  Pallas kernels: 41.4 us -> 36.9 us
    unnamed x35 -> x7, local copies, waits for them, and re-layouts: 9.59 us -> 4.12 us
    pallas_call x3 -> x1, Pallas kernels: 41.4 us -> 36.9 us  [body(): pl.pallas_call(functools.partial(fused_kernel, lat_count, lon_count), out...]
    slice x4 -> x0, local copies, waits for them, and re-layouts: 3.11 us -> none  [the longest x2 1.92 us: gather(): tracers[:, :, 0]]
    transpose x1 -> x0, local copies, waits for them, and re-layouts: 0.95 us -> none  [by_owner(): return jnp.moveaxis(edge, -3, 0)]
    another operation x5 -> x0, local copies, waits for them, and re-layouts: 0.8 us -> none  [the longest x1 0.64 us: by_owner(): edge = edge.reshape(edge.shape[:-2] + (lon_count, per, columns))]
where the time goes in v2:
time: 41.2 us; the launch traced here: 41 us
  Pallas kernels  36.9 us (90%)
  local copies, waits for them, and re-layouts  4.12 us (10%)
    pallas_call x1, Pallas kernels, body(): pl.pallas_call(functools.partial(fused_kernel, lat_count, lon_count), out...  36.9 us
    unnamed x7, local copies, waits for them, and re-layouts  4.12 us

profile of v2, /device:TPU:1, one launch (start us, length us, event | category | flops | bytes accessed | tf_op | source)
XLA Modules:
  0.0 41.0 jit_solution(16892257999854897098)
XLA Ops:
  0.0 0.0 copy-start
  0.0 0.7 %copy-done = s32[8,4]{0,1:T(4,128)S(1)} copy-done((s32[8,4]{0,1:T(4,128)S(1)}, s32[8,4]{0,1:T(4,128)}, u32[]{:S(2)}) %copy-start) | copy-done | bytes 152
  0.7 0.0 copy-start.1
  0.7 0.7 %copy.12.zs_in = s32[8,4]{1,0:T(8,128)} copy(s32[8,4]{0,1:T(4,128)S(1)} %copy-done) | data formatting | bytes 256 | tf_op args[2]
  1.4 0.0 copy-done.1
  1.4 0.7 %copy.13.zf_in = f32[8,4]{1,0:T(8,128)} copy(f32[8,4]{0,1:T(4,128)S(1)} %copy-done.1) | data formatting | bytes 256 | tf_op args[3]
  2.0 36.9 %shard_map.109 = f32[4,8,4,1440]{3,2,1,0:T(4,128)} custom-call(f32[4,8,4,1440]{3,2,1,0:T(4,128)} %tr.1, f32[8,4,1440]{2,1,0:T(4,128)} %cour.1, s32[8,4]{1,0:T(8,128)} %copy.12.zs_in, f32[8,4]{1,0:T(8,128)} %copy.13.zf_in, s32[2,128]{1,0:T(2,128)} %bitcast.2, f32[2,128]{1,0:T(2,128)} %bitcast.3, f32[2,23,128]{2,1,0:T(8,128)} %constant.10.clone.twid_in, ...), custom_call_target="tpu_custom_call" | custom-call | tf_op jit(solution)/shard_map/pallas_call | solution.py:423
  38.9 2.1 %copy.15 = f32[4,8,4,1440]{3,2,1,0:T(4,128)} copy(f32[4,8,4,1440]{3,2,1,0:T(4,128)} %shard_map.109) | data formatting | bytes 1474560
Async XLA Ops:
  0.0 0.7 %copy-start = (s32[8,4]{0,1:T(4,128)S(1)}, s32[8,4]{0,1:T(4,128)}, u32[]{:S(2)}) copy-start(s32[8,4]{0,1:T(4,128)} %param.13) | copy-start | bytes 388
  0.7 0.7 %copy-start.1 = (f32[8,4]{0,1:T(4,128)S(1)}, f32[8,4]{0,1:T(4,128)}, u32[]{:S(2)}) copy-start(f32[8,4]{0,1:T(4,128)} %param.14) | copy-start | bytes 388

commit v3 on v2

--- a/solution.py
+++ b/solution.py
@@ -243,11 +243,27 @@
         return pltpu.make_async_copy(parts.at[lon, t], out.at[t, mine], b_local.at[t])
 
     barrier = pltpu.get_barrier_semaphore()
-    friends = [{"lat": lat, "lon": peer} for peer in peers]
-    friends += [{"lat": up, "lon": across}, {"lat": down, "lon": across}]
-    for friend in friends:
+    has_north = (2 * lat_count - 3 - lat) // (lat_count - 1)
+    has_south = (lat + lat_count - 2) // (lat_count - 1)
+    sides = [(has_north == 1, {"lat": up, "lon": across}), (has_south == 1, {"lat": down, "lon": across})]
+
+    def signal(friend):
         pl.semaphore_signal(barrier, inc=1, device_id=friend, device_id_type=MESH)
-    pl.semaphore_wait(barrier, len(friends))
+
+    for peer in peers:
+        signal({"lat": lat, "lon": peer})
+    for there, friend in sides:
+        pl.when(there)(functools.partial(signal, friend))
+    pl.semaphore_wait(barrier, len(peers) + has_north + has_south)
+    north_there, south_there = sides[0][0], sides[1][0]
+
+    def start_rims(t, k):
+        north, south = rims(t, k)
+        pl.when(north_there)(north.start)
+        pl.when(south_there)(south.start)
+
+    def start_rim_speed(k):
+        pl.when(south_there)(rim_speed(k).start)
 
     for m in (1, 2, 0):
         speeds(m).start()
@@ -259,18 +275,16 @@
 
     def relay(t):
         cells(t, 0).wait_recv()
-        for copy in rims(t, 0):
-            copy.start()
+        start_rims(t, 0)
         cells(t, 1).wait_recv()
         cells(t, 2).wait_recv()
-        for copy in rims(t, 1):
-            copy.start()
+        start_rims(t, 1)
 
     speeds(0).wait_recv()
-    rim_speed(0).start()
+    start_rim_speed(0)
     speeds(1).wait_recv()
     speeds(2).wait_recv()
-    rim_speed(1).start()
+    start_rim_speed(1)
     relay(0)
 
     shape = (8, LANES)
@@ -279,13 +293,12 @@
     lane = lax.broadcasted_iota(jnp.int32, shape, 1)
 
     def own_levels(ref):
-        rows = ref[mine].astype(jnp.float32)
-        wide = jnp.concatenate(
-            [jnp.broadcast_to(rows[i : i + 1], (4, row_count)) for i in range(2)], axis=0
-        )
+        rows = ref[...].astype(jnp.float32)
+        wide = jnp.concatenate([rows, rows], axis=0)
         a = lax.broadcasted_iota(jnp.int32, wide.shape, 0)
         b = lax.broadcasted_iota(jnp.int32, wide.shape, 1)
-        value = jnp.sum(jnp.where(b == (a & 3), wide, 0.0), axis=1, keepdims=True)
+        at = 2 * lax.rem(lon + flip, lon_count) + (a // 4)
+        value = jnp.sum(jnp.where(b == at, wide, 0.0), axis=1, keepdims=True)
         return jnp.broadcast_to(value, shape)
 
     def own_rows(ref):
@@ -318,8 +331,9 @@
             relay(t + 1)
 
         for k in range(2):
-            for copy in rims(t, k):
-                copy.wait_recv()
+            north, south = rims(t, k)
+            pl.when(south_there)(north.wait_recv)
+            pl.when(north_there)(south.wait_recv)
         for seg in range(lon_count):
             x = stacked(got_t, seg, t)
             c = stacked(got_c, seg)
@@ -384,24 +398,38 @@
         return carry
 
     for k in range(2):
-        rim_speed(k).wait_recv()
+        pl.when(north_there)(rim_speed(k).wait_recv)
     lax.fori_loop(0, tracer_count, tracer, 0)
 
     for m in range(3):
         speeds(m).wait_send()
     for k in range(2):
-        rim_speed(k).wait_send()
+        pl.when(south_there)(rim_speed(k).wait_send)
     for t in range(tracer_count):
         for m in range(3):
             cells(t, m).wait_send()
         for k in range(2):
-            for copy in rims(t, k):
-                copy.wait_send()
+            north, south = rims(t, k)
+            pl.when(north_there)(north.wait_send)
+            pl.when(south_there)(south.wait_send)
         for m in range(3):
             reply(t, m).wait_send()
             back = reply(t, m)
             back.wait_recv()
         keep(t).wait()
+
+
+def deliver_kernel(held, out, room, sems):
+    count = held.shape[0]
+    reads = [pltpu.make_async_copy(held.at[t], room.at[t], sems.at[0, t]) for t in range(count)]
+    writes = [pltpu.make_async_copy(room.at[t], out.at[t], sems.at[1, t]) for t in range(count)]
+    for read in reads:
+        read.start()
+    for read, write in zip(reads, writes):
+        read.wait()
+        write.start()
+    for write in writes:
+        write.wait()
 
 
 def body(tracers, merid_courant, zonal_shift, zonal_fraction, cutoff, damping):
@@ -411,7 +439,7 @@
     per = level_count // lon_count
     twid, kabs, scale, fwd, inv = tables(columns * lon_count)
     operands = (
-        tracers, merid_courant, zonal_shift, zonal_fraction,
+        tracers, merid_courant, zonal_shift.T, zonal_fraction.T,
         cutoff.reshape(-1, LANES), damping.reshape(-1, LANES),
         jnp.asarray(twid), jnp.asarray(kabs), jnp.asarray(scale), *halves(fwd), *halves(inv),
     )
@@ -420,7 +448,7 @@
     f32 = jnp.float32
     small = [pltpu.VMEM(a.shape, a.dtype) for a in operands[2:]]
     dma = pltpu.SemaphoreType.DMA
-    return pl.pallas_call(
+    result = pl.pallas_call(
         functools.partial(fused_kernel, lat_count, lon_count),
         out_shape=jax.ShapeDtypeStruct(tracers.shape, f32),
         in_specs=[any_space] * len(operands),
@@ -446,6 +474,13 @@
         ],
         compiler_params=pltpu.CompilerParams(collective_id=0, has_side_effects=True),
     )(*operands)
+    return pl.pallas_call(
+        deliver_kernel,
+        out_shape=jax.ShapeDtypeStruct(tracers.shape, f32),
+        in_specs=[any_space],
+        out_specs=any_space,
+        scratch_shapes=[pltpu.VMEM(tracers.shape, f32), dma((2, tracer_count))],
+    )(result)
 
 
 def solution(mesh):

time: 41.2 us -> 33.5 us (0.81)
  the two profiles are of different devices: /device:TPU:1 before, /device:TPU:119 now
where the time goes in v3:
time: 33.5 us; the launch traced here: 33.4 us
  Pallas kernels  33.4 us (100%)
    pallas_call x1, Pallas kernels, body(): pl.pallas_call(functools.partial(fused_kernel, lat_count, lon_count), out...  31.4 us
    pallas_call x1, Pallas kernels, body(): pl.pallas_call(deliver_kernel, out_shape=jax.ShapeDtypeStruct(tracers.sha...  1.96 us

profile of v3, /device:TPU:119, one launch (start us, length us, event | category | flops | bytes accessed | tf_op | source)
XLA Modules:
  0.0 33.4 jit_solution(8257818154600416168)
XLA Ops:
  0.0 31.4 %shard_map.109.held = f32[4,8,4,1440]{3,2,1,0:T(4,128)} custom-call(f32[4,8,4,1440]{3,2,1,0:T(4,128)} %tr.1, f32[8,4,1440]{2,1,0:T(4,128)} %cour.1, s32[4,8]{1,0:T(4,128)} %bitcast.4, f32[4,8]{1,0:T(4,128)} %bitcast.5, s32[2,128]{1,0:T(2,128)} %bitcast.6, f32[2,128]{1,0:T(2,128)} %bitcast.7, f32[2,23,128]{2,1,0:T(8,128)} %constant.10.clone.twid_in, ...), custom_call_target="tpu_custom_call" | custom-call | tf_op jit(solution)/shard_map/pallas_call | solution.py:451
  31.4 2.0 %shard_map.110 = f32[4,8,4,1440]{3,2,1,0:T(4,128)} custom-call(f32[4,8,4,1440]{3,2,1,0:T(4,128)} %shard_map.109.held), custom_call_target="tpu_custom_call" | custom-call | tf_op jit(solution)/shard_map/pallas_call | solution.py:477

commit v4 on v3

--- a/solution.py
+++ b/solution.py
@@ -419,17 +419,10 @@
         keep(t).wait()
 
 
-def deliver_kernel(held, out, room, sems):
-    count = held.shape[0]
-    reads = [pltpu.make_async_copy(held.at[t], room.at[t], sems.at[0, t]) for t in range(count)]
-    writes = [pltpu.make_async_copy(room.at[t], out.at[t], sems.at[1, t]) for t in range(count)]
-    for read in reads:
-        read.start()
-    for read, write in zip(reads, writes):
-        read.wait()
-        write.start()
-    for write in writes:
-        write.wait()
+def deliver_kernel(held, out, sem):
+    copy = pltpu.make_async_copy(held, out, sem.at[0])
+    copy.start()
+    copy.wait()
 
 
 def body(tracers, merid_courant, zonal_shift, zonal_fraction, cutoff, damping):
@@ -444,6 +437,7 @@
         jnp.asarray(twid), jnp.asarray(kabs), jnp.asarray(scale), *halves(fwd), *halves(inv),
     )
     any_space = pl.BlockSpec(memory_space=pl.ANY)
+    operands = tuple(pltpu.with_memory_space_constraint(a, pltpu.HBM) for a in operands)
     tile = (per, row_count, columns)
     f32 = jnp.float32
     small = [pltpu.VMEM(a.shape, a.dtype) for a in operands[2:]]
@@ -452,7 +446,7 @@
         functools.partial(fused_kernel, lat_count, lon_count),
         out_shape=jax.ShapeDtypeStruct(tracers.shape, f32),
         in_specs=[any_space] * len(operands),
-        out_specs=any_space,
+        out_specs=pl.BlockSpec(memory_space=pltpu.VMEM),
         scratch_shapes=[
             pltpu.VMEM((lon_count, tracer_count) + tile, f32),
             pltpu.VMEM((lon_count,) + tile, f32),
@@ -472,14 +466,17 @@
             dma((tracer_count,)),
             dma((len(operands),)),
         ],
-        compiler_params=pltpu.CompilerParams(collective_id=0, has_side_effects=True),
+        compiler_params=pltpu.CompilerParams(
+            collective_id=0, has_side_effects=True, vmem_limit_bytes=16 << 20
+        ),
     )(*operands)
     return pl.pallas_call(
         deliver_kernel,
         out_shape=jax.ShapeDtypeStruct(tracers.shape, f32),
-        in_specs=[any_space],
+        in_specs=[pl.BlockSpec(memory_space=pltpu.VMEM)],
         out_specs=any_space,
-        scratch_shapes=[pltpu.VMEM(tracers.shape, f32), dma((2, tracer_count))],
+        scratch_shapes=[dma((1,))],
+        compiler_params=pltpu.CompilerParams(vmem_limit_bytes=4 << 20),
     )(result)
 
 

time: 33.5 us -> 32.4 us (0.967)
  Pallas kernels: 33.4 us -> 32.3 us
    pallas_call x1, Pallas kernels: 1.96 us -> 0.89 us  [body(): pl.pallas_call(deliver_kernel, out_shape=jax.ShapeDtypeStruct(tracers.sha...]
where the time goes in v4:
time: 32.4 us; the launch traced here: 32.3 us
  Pallas kernels  32.3 us (100%)
    pallas_call x1, Pallas kernels, body(): pl.pallas_call(functools.partial(fused_kernel, lat_count, lon_count), out...  31.4 us
    pallas_call x1, Pallas kernels, body(): pl.pallas_call(deliver_kernel, out_shape=jax.ShapeDtypeStruct(tracers.sha...  0.89 us

profile of v4, /device:TPU:119, one launch (start us, length us, event | category | flops | bytes accessed | tf_op | source)
XLA Modules:
  0.0 32.3 jit_solution(11885300564519459094)
XLA Ops:
  0.0 31.4 %shard_map.109.held = f32[4,8,4,1440]{3,2,1,0:T(4,128)S(1)} custom-call(f32[4,8,4,1440]{3,2,1,0:T(4,128)} %tr.1, f32[8,4,1440]{2,1,0:T(4,128)} %cour.1, s32[4,8]{1,0:T(4,128)} %bitcast.4, f32[4,8]{1,0:T(4,128)} %bitcast.5, s32[2,128]{1,0:T(2,128)} %bitcast.6, f32[2,128]{1,0:T(2,128)} %bitcast.7, f32[2,23,128]{2,1,0:T(8,128)} %constant.10.clone.twid_in, ...), custom_call_target="tpu_custom_call" | custom-call | tf_op jit(solution)/shard_map/pallas_call | solution.py:445
  31.4 0.9 %shard_map.110 = f32[4,8,4,1440]{3,2,1,0:T(4,128)} custom-call(f32[4,8,4,1440]{3,2,1,0:T(4,128)S(1)} %shard_map.109.held), custom_call_target="tpu_custom_call" | custom-call | tf_op jit(solution)/shard_map/pallas_call | solution.py:473

commit v5 on v4

--- a/solution.py
+++ b/solution.py
@@ -178,9 +178,6 @@
     peers = [lon + 1 - 2 * lax.rem(lon, 2), lax.rem(lon + 2, lon_count), lon_count - 1 - lon]
     levels = [pl.ds(2 * lax.rem(peer + flip, lon_count), 2) for peer in peers]
     mine = pl.ds(2 * lax.rem(lon + flip, lon_count), 2)
-    across = peers[1]
-    near = 2 * (lon // 2)
-    pairs = [near, 2 - near]
 
     staged = [
         (tr.at[:, mine], got_t.at[lon]), (cour.at[mine], got_c.at[lon]),
@@ -212,26 +209,39 @@
             {"lat": lat, "lon": peers[m]},
         )
 
-    def rims(t, k):
-        both = pl.ds(pairs[k], 2)
-        north = remote(
-            got_t.at[both, t, :, pl.ds(row_count - 1, 1)],
-            halo_t.at[both, t, :, pl.ds(row_count - 1, 1)],
-            h_send.at[t, k], h_recv.at[t, k], {"lat": up, "lon": across},
+    last = pl.ds(row_count - 1, 1)
+    first = pl.ds(0, 1)
+    far = pl.ds(2 - 2 * (lon // 2), 2)
+    direct = [(mine, peers[1]), (levels[0], peers[2])]
+
+    def rims(t):
+        copies = []
+        for j, (owned, owner) in enumerate(direct):
+            copies.append((
+                remote(tr.at[t, owned, last], halo_t.at[lon, t, :, last],
+                       h_send.at[t, j], h_recv.at[t, j], {"lat": up, "lon": owner}),
+                remote(tr.at[t, owned, first], halo_t.at[lon, t, :, first],
+                       h_send.at[t, j + 3], h_recv.at[t, j + 3], {"lat": down, "lon": owner}),
+            ))
+        copies.append((
+            remote(got_t.at[far, t, :, last], halo_t.at[far, t, :, last],
+                   h_send.at[t, 2], h_recv.at[t, 2], {"lat": up, "lon": peers[1]}),
+            remote(got_t.at[far, t, :, first], halo_t.at[far, t, :, first],
+                   h_send.at[t, 5], h_recv.at[t, 5], {"lat": down, "lon": peers[1]}),
+        ))
+        return copies
+
+    def rim_speeds():
+        copies = [
+            remote(cour.at[owned, first], halo_c.at[lon, :, first],
+                   hc_send.at[j], hc_recv.at[j], {"lat": down, "lon": owner})
+            for j, (owned, owner) in enumerate(direct)
+        ]
+        copies.append(
+            remote(got_c.at[far, :, first], halo_c.at[far, :, first],
+                   hc_send.at[2], hc_recv.at[2], {"lat": down, "lon": peers[1]})
         )
-        south = remote(
-            got_t.at[both, t, :, pl.ds(0, 1)],
-            halo_t.at[both, t, :, pl.ds(0, 1)],
-            h_send.at[t, k + 2], h_recv.at[t, k + 2], {"lat": down, "lon": across},
-        )
-        return north, south
-
-    def rim_speed(k):
-        both = pl.ds(pairs[k], 2)
-        return remote(
-            got_c.at[both, :, pl.ds(0, 1)], halo_c.at[both, :, pl.ds(0, 1)],
-            hc_send.at[k], hc_recv.at[k], {"lat": down, "lon": across},
-        )
+        return copies
 
     def reply(t, m):
         return remote(
@@ -245,47 +255,56 @@
     barrier = pltpu.get_barrier_semaphore()
     has_north = (2 * lat_count - 3 - lat) // (lat_count - 1)
     has_south = (lat + lat_count - 2) // (lat_count - 1)
-    sides = [(has_north == 1, {"lat": up, "lon": across}), (has_south == 1, {"lat": down, "lon": across})]
+    north_there, south_there = has_north == 1, has_south == 1
 
     def signal(friend):
         pl.semaphore_signal(barrier, inc=1, device_id=friend, device_id_type=MESH)
 
     for peer in peers:
         signal({"lat": lat, "lon": peer})
-    for there, friend in sides:
-        pl.when(there)(functools.partial(signal, friend))
-    pl.semaphore_wait(barrier, len(peers) + has_north + has_south)
-    north_there, south_there = sides[0][0], sides[1][0]
-
-    def start_rims(t, k):
-        north, south = rims(t, k)
-        pl.when(north_there)(north.start)
-        pl.when(south_there)(south.start)
-
-    def start_rim_speed(k):
-        pl.when(south_there)(rim_speed(k).start)
+    for owner in peers[1:]:
+        pl.when(north_there)(functools.partial(signal, {"lat": up, "lon": owner}))
+        pl.when(south_there)(functools.partial(signal, {"lat": down, "lon": owner}))
+    pl.semaphore_wait(barrier, len(peers) + 2 * has_north + 2 * has_south)
+
+    def each_rim(north_act, south_act, copies):
+        @pl.when(north_act[0])
+        def _():
+            for north, _ in copies:
+                getattr(north, north_act[1])()
+
+        @pl.when(south_act[0])
+        def _():
+            for _, south in copies:
+                getattr(south, south_act[1])()
+
+    def start_rims(copies):
+        each_rim((north_there, "start"), (south_there, "start"), copies)
+
+    @pl.when(south_there)
+    def _():
+        for copy in rim_speeds()[:2]:
+            copy.start()
 
     for m in (1, 2, 0):
         speeds(m).start()
     for t in range(tracer_count):
+        start_rims(rims(t)[:2])
         for m in (1, 2, 0):
             cells(t, m).start()
     for copy in staged:
         copy.wait()
 
     def relay(t):
-        cells(t, 0).wait_recv()
-        start_rims(t, 0)
         cells(t, 1).wait_recv()
         cells(t, 2).wait_recv()
-        start_rims(t, 1)
-
-    speeds(0).wait_recv()
-    start_rim_speed(0)
+        start_rims(rims(t)[2:])
+
     speeds(1).wait_recv()
     speeds(2).wait_recv()
-    start_rim_speed(1)
+    pl.when(south_there)(rim_speeds()[2].start)
     relay(0)
+    speeds(0).wait_recv()
 
     shape = (8, LANES)
     sub = lax.broadcasted_iota(jnp.int32, (8, columns), 0)
@@ -316,9 +335,8 @@
     face = lat * row_count + (sub & 3)
     open_s8 = face > 0
     open_n8 = face + 1 < lat_count * row_count
-    band = lat + 0 * lane
     quarter = lat_count // 4
-    cap8 = (band < quarter) | (band >= lat_count - quarter)
+    in_cap = (lat < quarter) | (lat >= lat_count - quarter)
     fold0, fold1 = (lane - s0) & (LANES - 1), (lane - s1) & (LANES - 1)
     own0, own1 = lane >= s0, lane >= s1
 
@@ -330,10 +348,8 @@
         def _():
             relay(t + 1)
 
-        for k in range(2):
-            north, south = rims(t, k)
-            pl.when(south_there)(north.wait_recv)
-            pl.when(north_there)(south.wait_recv)
+        cells(t, 0).wait_recv()
+        each_rim((south_there, "wait_recv"), (north_there, "wait_recv"), rims(t))
         for seg in range(lon_count):
             x = stacked(got_t, seg, t)
             c = stacked(got_c, seg)
@@ -355,39 +371,53 @@
                 jnp.take_along_axis(tile, fold1, axis=1),
             )
 
-        previous = gathered(PTS - 1)
-        x = []
-        for p in range(PTS):
-            now = gathered(p)
-            current = jnp.where(own0, now[0], previous[0])
-            earlier = jnp.where(own1, now[1], previous[1])
-            value = (1.0 - here) * current + here * earlier
-            moved[:, p * LANES : (p + 1) * LANES] = value
-            x.append(value)
-            previous = now
-        for r, (re, im) in enumerate(forward45(x)):
-            tc, ts = twid[0, r : r + 1], twid[1, r : r + 1]
-            if im is None:
-                spec[8 * r : 8 * r + 8, :LANES] = re * tc
-                spec[8 * r : 8 * r + 8, LANES:] = -(re * ts)
-            else:
-                spec[8 * r : 8 * r + 8, :LANES] = re * tc + im * ts
-                spec[8 * r : 8 * r + 8, LANES:] = im * tc - re * ts
-        wave[...] = split_dot(spec[...], fwd_h[...], fwd_l[...])
-        for r in range(HALF):
-            weight = jnp.where(kabs[r : r + 1] <= cut8, scale[r : r + 1], 0.0)
-            wave[8 * r : 8 * r + 8, :] = wave[8 * r : 8 * r + 8, :] * weight
-        spec[...] = split_dot(wave[...], inv_h[...], inv_l[...])
-        v = []
-        for r in range(HALF):
-            tc, ts = twid[0, r : r + 1], twid[1, r : r + 1]
-            re, im = spec[8 * r : 8 * r + 8, :LANES], spec[8 * r : 8 * r + 8, LANES:]
-            v.append((re * tc - im * ts, re * ts + im * tc))
-        for p, low in enumerate(inverse45(v)):
-            cols = slice(p * LANES, (p + 1) * LANES)
-            shifted = moved[:, cols]
-            filtered = damp8 * shifted + (1.0 - damp8) * low
-            line[:, cols] = jnp.where(cap8, filtered, shifted)
+        @pl.when(in_cap)
+        def _():
+            previous = gathered(PTS - 1)
+            x = []
+            for p in range(PTS):
+                now = gathered(p)
+                current = jnp.where(own0, now[0], previous[0])
+                earlier = jnp.where(own1, now[1], previous[1])
+                value = (1.0 - here) * current + here * earlier
+                moved[:, p * LANES : (p + 1) * LANES] = value
+                x.append(value)
+                previous = now
+            for r, (re, im) in enumerate(forward45(x)):
+                tc, ts = twid[0, r : r + 1], twid[1, r : r + 1]
+                if im is None:
+                    spec[8 * r : 8 * r + 8, :LANES] = re * tc
+                    spec[8 * r : 8 * r + 8, LANES:] = -(re * ts)
+                else:
+                    spec[8 * r : 8 * r + 8, :LANES] = re * tc + im * ts
+                    spec[8 * r : 8 * r + 8, LANES:] = im * tc - re * ts
+            wave[...] = split_dot(spec[...], fwd_h[...], fwd_l[...])
+            for r in range(HALF):
+                weight = jnp.where(kabs[r : r + 1] <= cut8, scale[r : r + 1], 0.0)
+                wave[8 * r : 8 * r + 8, :] = wave[8 * r : 8 * r + 8, :] * weight
+            spec[...] = split_dot(wave[...], inv_h[...], inv_l[...])
+            v = []
+            for r in range(HALF):
+                tc, ts = twid[0, r : r + 1], twid[1, r : r + 1]
+                re, im = spec[8 * r : 8 * r + 8, :LANES], spec[8 * r : 8 * r + 8, LANES:]
+                v.append((re * tc - im * ts, re * ts + im * tc))
+            for p, low in enumerate(inverse45(v)):
+                cols = slice(p * LANES, (p + 1) * LANES)
+                shifted = moved[:, cols]
+                filtered = damp8 * shifted + (1.0 - damp8) * low
+                line[:, cols] = filtered
+
+        @pl.when(jnp.logical_not(in_cap))
+        def _():
+            previous = gathered(PTS - 1)
+            for p in range(PTS):
+                now = gathered(p)
+                current = jnp.where(own0, now[0], previous[0])
+                earlier = jnp.where(own1, now[1], previous[1])
+                moved[:, p * LANES : (p + 1) * LANES] = (1.0 - here) * current + here * earlier
+                previous = now
+            line[...] = moved[...]
+
         for seg in range(lon_count):
             value = line[:, seg * columns : (seg + 1) * columns]
             parts[seg, t, 0] = value[:4]
@@ -397,21 +427,25 @@
         keep(t).start()
         return carry
 
-    for k in range(2):
-        pl.when(north_there)(rim_speed(k).wait_recv)
+    @pl.when(north_there)
+    def _():
+        for copy in rim_speeds():
+            copy.wait_recv()
+
     lax.fori_loop(0, tracer_count, tracer, 0)
 
     for m in range(3):
         speeds(m).wait_send()
-    for k in range(2):
-        pl.when(south_there)(rim_speed(k).wait_send)
+
+    @pl.when(south_there)
+    def _():
+        for copy in rim_speeds():
+            copy.wait_send()
+
     for t in range(tracer_count):
         for m in range(3):
             cells(t, m).wait_send()
-        for k in range(2):
-            north, south = rims(t, k)
-            pl.when(north_there)(north.wait_send)
-            pl.when(south_there)(south.wait_send)
+        each_rim((north_there, "wait_send"), (south_there, "wait_send"), rims(t))
         for m in range(3):
             reply(t, m).wait_send()
             back = reply(t, m)
@@ -460,8 +494,8 @@
             pltpu.VMEM((HALF * 8, LANES), f32),
             dma((tracer_count, 3)), dma((tracer_count, 3)),
             dma((3,)), dma((3,)),
-            dma((tracer_count, 4)), dma((tracer_count, 4)),
-            dma((2,)), dma((2,)),
+            dma((tracer_count, 6)), dma((tracer_count, 6)),
+            dma((3,)), dma((3,)),
             dma((tracer_count, 3)), dma((tracer_count, 3)),
             dma((tracer_count,)),
             dma((len(operands),)),

time: 32.4 us -> 30.5 us (0.941)
  the two profiles are of different devices: /device:TPU:119 before, /device:TPU:225 now
where the time goes in v5:
time: 30.5 us; the launch traced here: 30.4 us
  Pallas kernels  30.4 us (100%)
    pallas_call x1, Pallas kernels, body(): pl.pallas_call(functools.partial(fused_kernel, lat_count, lon_count), out...  29.5 us
    pallas_call x1, Pallas kernels, body(): pl.pallas_call(deliver_kernel, out_shape=jax.ShapeDtypeStruct(tracers.sha...  0.89 us

profile of v5, /device:TPU:225, one launch (start us, length us, event | category | flops | bytes accessed | tf_op | source)
XLA Modules:
  0.0 30.4 jit_solution(15343330810429073385)
XLA Ops:
  0.0 29.5 %shard_map.109.held = f32[4,8,4,1440]{3,2,1,0:T(4,128)S(1)} custom-call(f32[4,8,4,1440]{3,2,1,0:T(4,128)} %tr.1, f32[8,4,1440]{2,1,0:T(4,128)} %cour.1, s32[4,8]{1,0:T(4,128)} %bitcast.4, f32[4,8]{1,0:T(4,128)} %bitcast.5, s32[2,128]{1,0:T(2,128)} %bitcast.6, f32[2,128]{1,0:T(2,128)} %bitcast.7, f32[2,23,128]{2,1,0:T(8,128)} %constant.10.clone.twid_in, ...), custom_call_target="tpu_custom_call" | custom-call | tf_op jit(solution)/shard_map/pallas_call | solution.py:479
  29.5 0.9 %shard_map.110 = f32[4,8,4,1440]{3,2,1,0:T(4,128)} custom-call(f32[4,8,4,1440]{3,2,1,0:T(4,128)S(1)} %shard_map.109.held), custom_call_target="tpu_custom_call" | custom-call | tf_op jit(solution)/shard_map/pallas_call | solution.py:507

commit v6 on v5

--- a/solution.py
+++ b/solution.py
@@ -167,7 +167,7 @@
     got_t, got_c, halo_t, halo_c, parts,
     zs, zf, cut, damp, twid, kabs, scale, fwd_h, fwd_l, inv_h, inv_l,
     line, moved, spec, wave,
-    t_send, t_recv, c_send, c_recv, h_send, h_recv, hc_send, hc_recv, b_send, b_recv, b_local, local,
+    t_send, t_recv, c_send, c_recv, h_send, h_recv, hc_send, hc_recv, b_send, b_recv, b_local, local, ready,
 ):
     tracer_count, _, row_count, columns = tr.shape
     lat = lax.axis_index("lat")
@@ -243,9 +243,11 @@
         )
         return copies
 
-    def reply(t, m):
+    def reply(t, m, piece):
+        rows = (pl.ds(1, row_count - 2), first, last)[piece]
         return remote(
-            parts.at[peers[m], t], out.at[t, mine], b_send.at[t, m], b_recv.at[t, m],
+            parts.at[peers[m], t, :, rows], out.at[t, mine, rows],
+            b_send.at[t, 3 * m + piece], b_recv.at[t, 3 * m + piece],
             {"lat": lat, "lon": peers[m]},
         )
 
@@ -262,10 +264,24 @@
 
     for peer in peers:
         signal({"lat": lat, "lon": peer})
-    for owner in peers[1:]:
-        pl.when(north_there)(functools.partial(signal, {"lat": up, "lon": owner}))
-        pl.when(south_there)(functools.partial(signal, {"lat": down, "lon": owner}))
-    pl.semaphore_wait(barrier, len(peers) + 2 * has_north + 2 * has_south)
+    core = lax.rem(lon, 2)
+    keeper = peers[1] + 1 - core
+    pl.when(north_there)(functools.partial(signal, {"lat": up, "lon": keeper}))
+    pl.when(south_there)(functools.partial(signal, {"lat": down, "lon": keeper}))
+    pl.semaphore_wait(barrier, len(peers) + core * (2 * has_north + 2 * has_south))
+    for m in (1, 2, 0):
+        speeds(m).start()
+    for t in range(tracer_count):
+        for m in (1, 2, 0):
+            cells(t, m).start()
+
+    @pl.when(core == 1)
+    def _():
+        pl.semaphore_signal(ready, inc=1, device_id={"lat": lat, "lon": peers[0]}, device_id_type=MESH)
+
+    @pl.when(core == 0)
+    def _():
+        pl.semaphore_wait(ready, 1)
 
     def each_rim(north_act, south_act, copies):
         @pl.when(north_act[0])
@@ -286,12 +302,8 @@
         for copy in rim_speeds()[:2]:
             copy.start()
 
-    for m in (1, 2, 0):
-        speeds(m).start()
     for t in range(tracer_count):
         start_rims(rims(t)[:2])
-        for m in (1, 2, 0):
-            cells(t, m).start()
     for copy in staged:
         copy.wait()
 
@@ -303,7 +315,6 @@
     speeds(1).wait_recv()
     speeds(2).wait_recv()
     pl.when(south_there)(rim_speeds()[2].start)
-    relay(0)
     speeds(0).wait_recv()
 
     shape = (8, LANES)
@@ -327,42 +338,57 @@
         value = jnp.sum(jnp.where(lane == at, wide, 0.0), axis=1, keepdims=True)
         return jnp.broadcast_to(value, shape)
 
-    s0 = own_levels(zs).astype(jnp.int32)
-    s1 = s0 + 1
-    here = own_levels(zf)
-    cut8 = own_rows(cut).astype(jnp.int32)
-    damp8 = own_rows(damp)
     face = lat * row_count + (sub & 3)
     open_s8 = face > 0
     open_n8 = face + 1 < lat_count * row_count
     quarter = lat_count // 4
     in_cap = (lat < quarter) | (lat >= lat_count - quarter)
-    fold0, fold1 = (lane - s0) & (LANES - 1), (lane - s1) & (LANES - 1)
-    own0, own1 = lane >= s0, lane >= s1
+    given = (own_levels(zs), own_levels(zf), own_rows(cut), own_rows(damp))
+
+    def joined(edge, one, two):
+        inner = (lax.broadcasted_iota(jnp.int32, one.shape, 0) + 1) & 2
+        return jnp.where(inner == (0 if edge else 2), one, pltpu.roll(two, 2, 0))
 
     def stacked(ref, *at):
         return jnp.concatenate([ref[(*at, 0)], ref[(*at, 1)]], axis=0)
 
-    def tracer(t, carry):
-        @pl.when(t < tracer_count - 1)
-        def _():
-            relay(t + 1)
-
-        cells(t, 0).wait_recv()
-        each_rim((south_there, "wait_recv"), (north_there, "wait_recv"), rims(t))
-        for seg in range(lon_count):
-            x = stacked(got_t, seg, t)
-            c = stacked(got_c, seg)
+    def advected(seg, t, edge):
+        x = stacked(got_t, seg, t)
+        c = stacked(got_c, seg)
+        below = pltpu.roll(x, 1, 0)
+        if edge:
             rim = stacked(halo_t, seg, t)
             rim_c = stacked(halo_c, seg)
-            below = jnp.where((sub & 3) == 0, pltpu.roll(rim, 5, 0), pltpu.roll(x, 1, 0))
-            flux = jnp.maximum(c, 0.0) * below + jnp.minimum(c, 0.0) * x
+            below = jnp.where((sub & 3) == 0, pltpu.roll(rim, 5, 0), below)
+        flux = jnp.maximum(c, 0.0) * below + jnp.minimum(c, 0.0) * x
+        if edge:
             flux = jnp.where(open_s8, flux, 0.0)
+        top = pltpu.roll(flux, 7, 0)
+        if edge:
             hi, ch = pltpu.roll(rim, 3, 0), pltpu.roll(rim_c, 3, 0)
-            edge = jnp.maximum(ch, 0.0) * x + jnp.minimum(ch, 0.0) * hi
-            top = jnp.where((sub & 3) == 3, edge, pltpu.roll(flux, 7, 0))
+            top = jnp.where(
+                (sub & 3) == 3, jnp.maximum(ch, 0.0) * x + jnp.minimum(ch, 0.0) * hi, top
+            )
             top = jnp.where(open_n8, top, 0.0)
-            line[:, seg * columns : (seg + 1) * columns] = x + flux - top
+        return x + flux - top
+
+    def group(edge, pair, carry):
+        both = [2 * pair, 2 * pair + 1]
+        for t in both:
+            if edge:
+                each_rim((south_there, "wait_recv"), (north_there, "wait_recv"), rims(t))
+            else:
+                relay(t)
+                cells(t, 0).wait_recv()
+        s0, here, cut8, damp8 = [joined(edge, value, value) for value in given]
+        s0, cut8 = s0.astype(jnp.int32), cut8.astype(jnp.int32)
+        s1 = s0 + 1
+        fold0, fold1 = (lane - s0) & (LANES - 1), (lane - s1) & (LANES - 1)
+        own0, own1 = lane >= s0, lane >= s1
+        for seg in range(lon_count):
+            line[:, seg * columns : (seg + 1) * columns] = joined(
+                edge, advected(seg, both[0], edge), advected(seg, both[1], edge)
+            )
 
         def gathered(p):
             tile = line[:, p * LANES : (p + 1) * LANES]
@@ -420,19 +446,30 @@
 
         for seg in range(lon_count):
             value = line[:, seg * columns : (seg + 1) * columns]
-            parts[seg, t, 0] = value[:4]
-            parts[seg, t, 1] = value[4:]
-        for m in (1, 2, 0):
-            reply(t, m).start()
-        keep(t).start()
+            for t, rows in zip(both, (value, pltpu.roll(value, 6, 0))):
+                for level in range(2):
+                    tile = rows[4 * level : 4 * level + 4]
+                    if edge:
+                        parts[seg, t, level, 0:1] = tile[0:1]
+                        parts[seg, t, level, 3:4] = tile[3:4]
+                    else:
+                        parts[seg, t, level] = tile
+        for t in both:
+            for piece in ((1, 2) if edge else (0,)):
+                for m in (1, 2, 0):
+                    reply(t, m, piece).start()
+            if edge:
+                keep(t).start()
         return carry
+
+    lax.fori_loop(0, tracer_count // 2, functools.partial(group, False), 0)
 
     @pl.when(north_there)
     def _():
         for copy in rim_speeds():
             copy.wait_recv()
 
-    lax.fori_loop(0, tracer_count, tracer, 0)
+    lax.fori_loop(0, tracer_count // 2, functools.partial(group, True), 0)
 
     for m in range(3):
         speeds(m).wait_send()
@@ -447,9 +484,10 @@
             cells(t, m).wait_send()
         each_rim((north_there, "wait_send"), (south_there, "wait_send"), rims(t))
         for m in range(3):
-            reply(t, m).wait_send()
-            back = reply(t, m)
-            back.wait_recv()
+            for piece in range(3):
+                back = reply(t, m, piece)
+                back.wait_send()
+                back.wait_recv()
         keep(t).wait()
 
 
@@ -496,9 +534,10 @@
             dma((3,)), dma((3,)),
             dma((tracer_count, 6)), dma((tracer_count, 6)),
             dma((3,)), dma((3,)),
-            dma((tracer_count, 3)), dma((tracer_count, 3)),
+            dma((tracer_count, 9)), dma((tracer_count, 9)),
             dma((tracer_count,)),
             dma((len(operands),)),
+            pltpu.SemaphoreType.REGULAR,
         ],
         compiler_params=pltpu.CompilerParams(
             collective_id=0, has_side_effects=True, vmem_limit_bytes=16 << 20

time: 30.5 us -> 28.4 us (0.931)
  the two profiles are of different devices: /device:TPU:225 before, /device:TPU:201 now
where the time goes in v6:
time: 28.4 us
  Pallas kernels  28.3 us (100%)
    pallas_call x1, Pallas kernels, body(): pl.pallas_call(functools.partial(fused_kernel, lat_count, lon_count), out...  27.5 us
    pallas_call x1, Pallas kernels, body(): pl.pallas_call(deliver_kernel, out_shape=jax.ShapeDtypeStruct(tracers.sha...  0.89 us

profile of v6, /device:TPU:201, one launch (start us, length us, event | category | flops | bytes accessed | tf_op | source)
XLA Modules:
  0.0 28.4 jit_solution(5748421149178734415)
XLA Ops:
  0.0 27.5 %shard_map.109.held = f32[4,8,4,1440]{3,2,1,0:T(4,128)S(1)} custom-call(f32[4,8,4,1440]{3,2,1,0:T(4,128)} %tr.1, f32[8,4,1440]{2,1,0:T(4,128)} %cour.1, s32[4,8]{1,0:T(4,128)} %bitcast.4, f32[4,8]{1,0:T(4,128)} %bitcast.5, s32[2,128]{1,0:T(2,128)} %bitcast.6, f32[2,128]{1,0:T(2,128)} %bitcast.7, f32[2,23,128]{2,1,0:T(8,128)} %constant.10.clone.twid_in, ...), custom_call_target="tpu_custom_call" | custom-call | tf_op jit(solution)/shard_map/pallas_call | solution.py:517
  27.5 0.9 %shard_map.110 = f32[4,8,4,1440]{3,2,1,0:T(4,128)} custom-call(f32[4,8,4,1440]{3,2,1,0:T(4,128)S(1)} %shard_map.109.held), custom_call_target="tpu_custom_call" | custom-call | tf_op jit(solution)/shard_map/pallas_call | solution.py:546

commit v7 on v6

--- a/solution.py
+++ b/solution.py
@@ -197,9 +197,14 @@
             device_id=device, device_id_type=MESH,
         )
 
-    def cells(t, m):
+    last = pl.ds(row_count - 1, 1)
+    first = pl.ds(0, 1)
+    pieces = (pl.ds(1, row_count - 2), first, last)
+
+    def cells(t, m, piece):
         return remote(
-            tr.at[t, levels[m]], got_t.at[lon, t], t_send.at[t, m], t_recv.at[t, m],
+            tr.at[t, levels[m], pieces[piece]], got_t.at[lon, t, :, pieces[piece]],
+            t_send.at[t, 3 * m + piece], t_recv.at[t, 3 * m + piece],
             {"lat": lat, "lon": peers[m]},
         )
 
@@ -209,8 +214,6 @@
             {"lat": lat, "lon": peers[m]},
         )
 
-    last = pl.ds(row_count - 1, 1)
-    first = pl.ds(0, 1)
     far = pl.ds(2 - 2 * (lon // 2), 2)
     direct = [(mine, peers[1]), (levels[0], peers[2])]
 
@@ -244,7 +247,7 @@
         return copies
 
     def reply(t, m, piece):
-        rows = (pl.ds(1, row_count - 2), first, last)[piece]
+        rows = pieces[piece]
         return remote(
             parts.at[peers[m], t, :, rows], out.at[t, mine, rows],
             b_send.at[t, 3 * m + piece], b_recv.at[t, 3 * m + piece],
@@ -271,9 +274,11 @@
     pl.semaphore_wait(barrier, len(peers) + core * (2 * has_north + 2 * has_south))
     for m in (1, 2, 0):
         speeds(m).start()
-    for t in range(tracer_count):
-        for m in (1, 2, 0):
-            cells(t, m).start()
+    for group_of in ((0,), (1,), (2, 3)):
+        for piece in (1, 2, 0):
+            for t in group_of:
+                for m in (1, 2, 0):
+                    cells(t, m, piece).start()
 
     @pl.when(core == 1)
     def _():
@@ -308,8 +313,9 @@
         copy.wait()
 
     def relay(t):
-        cells(t, 1).wait_recv()
-        cells(t, 2).wait_recv()
+        for m in (1, 2):
+            for piece in (1, 2):
+                cells(t, m, piece).wait_recv()
         start_rims(rims(t)[2:])
 
     speeds(1).wait_recv()
@@ -374,12 +380,17 @@
 
     def group(edge, pair, carry):
         both = [2 * pair, 2 * pair + 1]
+        if not edge:
+            for t in both:
+                relay(t)
         for t in both:
             if edge:
                 each_rim((south_there, "wait_recv"), (north_there, "wait_recv"), rims(t))
             else:
-                relay(t)
-                cells(t, 0).wait_recv()
+                for m in range(3):
+                    cells(t, m, 0).wait_recv()
+                for piece in (1, 2):
+                    cells(t, 0, piece).wait_recv()
         s0, here, cut8, damp8 = [joined(edge, value, value) for value in given]
         s0, cut8 = s0.astype(jnp.int32), cut8.astype(jnp.int32)
         s1 = s0 + 1
@@ -481,7 +492,8 @@
 
     for t in range(tracer_count):
         for m in range(3):
-            cells(t, m).wait_send()
+            for piece in range(3):
+                cells(t, m, piece).wait_send()
         each_rim((north_there, "wait_send"), (south_there, "wait_send"), rims(t))
         for m in range(3):
             for piece in range(3):
@@ -530,7 +542,7 @@
             pltpu.VMEM((8, columns * lon_count), f32),
             pltpu.VMEM((HALF * 8, 2 * LANES), f32),
             pltpu.VMEM((HALF * 8, LANES), f32),
-            dma((tracer_count, 3)), dma((tracer_count, 3)),
+            dma((tracer_count, 9)), dma((tracer_count, 9)),
             dma((3,)), dma((3,)),
             dma((tracer_count, 6)), dma((tracer_count, 6)),
             dma((3,)), dma((3,)),

time: 28.4 us -> 28.1 us (0.989)
  the two profiles are of different devices: /device:TPU:201 before, /device:TPU:1 now
where the time goes in v7:
time: 28.1 us; the launch traced here: 28 us
  Pallas kernels  27.9 us (99%)
    pallas_call x1, Pallas kernels, body(): pl.pallas_call(functools.partial(fused_kernel, lat_count, lon_count), out...  27.1 us
    pallas_call x1, Pallas kernels, body(): pl.pallas_call(deliver_kernel, out_shape=jax.ShapeDtypeStruct(tracers.sha...  0.89 us

profile of v7, /device:TPU:1, one launch (start us, length us, event | category | flops | bytes accessed | tf_op | source)
XLA Modules:
  0.0 28.0 jit_solution(397728876869400372)
XLA Ops:
  0.0 27.1 %shard_map.109.held = f32[4,8,4,1440]{3,2,1,0:T(4,128)S(1)} custom-call(f32[4,8,4,1440]{3,2,1,0:T(4,128)} %tr.1, f32[8,4,1440]{2,1,0:T(4,128)} %cour.1, s32[4,8]{1,0:T(4,128)} %bitcast.4, f32[4,8]{1,0:T(4,128)} %bitcast.5, s32[2,128]{1,0:T(2,128)} %bitcast.6, f32[2,128]{1,0:T(2,128)} %bitcast.7, f32[2,23,128]{2,1,0:T(8,128)} %constant.10.clone.twid_in, ...), custom_call_target="tpu_custom_call" | custom-call | tf_op jit(solution)/shard_map/pallas_call | solution.py:529
  27.1 0.9 %shard_map.110 = f32[4,8,4,1440]{3,2,1,0:T(4,128)} custom-call(f32[4,8,4,1440]{3,2,1,0:T(4,128)S(1)} %shard_map.109.held), custom_call_target="tpu_custom_call" | custom-call | tf_op jit(solution)/shard_map/pallas_call | solution.py:558

commit v8 on v7

--- a/solution.py
+++ b/solution.py
@@ -378,11 +378,7 @@
             top = jnp.where(open_n8, top, 0.0)
         return x + flux - top
 
-    def group(edge, pair, carry):
-        both = [2 * pair, 2 * pair + 1]
-        if not edge:
-            for t in both:
-                relay(t)
+    def group(edge, both):
         for t in both:
             if edge:
                 each_rim((south_there, "wait_recv"), (north_there, "wait_recv"), rims(t))
@@ -391,15 +387,15 @@
                     cells(t, m, 0).wait_recv()
                 for piece in (1, 2):
                     cells(t, 0, piece).wait_recv()
-        s0, here, cut8, damp8 = [joined(edge, value, value) for value in given]
+        alone = len(both) == 1
+        s0, here, cut8, damp8 = [value if alone else joined(edge, value, value) for value in given]
         s0, cut8 = s0.astype(jnp.int32), cut8.astype(jnp.int32)
         s1 = s0 + 1
         fold0, fold1 = (lane - s0) & (LANES - 1), (lane - s1) & (LANES - 1)
         own0, own1 = lane >= s0, lane >= s1
         for seg in range(lon_count):
-            line[:, seg * columns : (seg + 1) * columns] = joined(
-                edge, advected(seg, both[0], edge), advected(seg, both[1], edge)
-            )
+            tiles = [advected(seg, t, edge) for t in both]
+            line[:, seg * columns : (seg + 1) * columns] = tiles[0] if alone else joined(edge, *tiles)
 
         def gathered(p):
             tile = line[:, p * LANES : (p + 1) * LANES]
@@ -457,7 +453,7 @@
 
         for seg in range(lon_count):
             value = line[:, seg * columns : (seg + 1) * columns]
-            for t, rows in zip(both, (value, pltpu.roll(value, 6, 0))):
+            for t, rows in zip(both, (value, None if alone else pltpu.roll(value, 6, 0))):
                 for level in range(2):
                     tile = rows[4 * level : 4 * level + 4]
                     if edge:
@@ -471,16 +467,25 @@
                     reply(t, m, piece).start()
             if edge:
                 keep(t).start()
-        return carry
-
-    lax.fori_loop(0, tracer_count // 2, functools.partial(group, False), 0)
+
+    for t in range(2):
+        relay(t)
+    group(False, [0, 1])
+    for t in range(2, tracer_count):
+        relay(t)
+
+    @pl.loop(2, tracer_count)
+    def _(t):
+        group(False, [t])
 
     @pl.when(north_there)
     def _():
         for copy in rim_speeds():
             copy.wait_recv()
 
-    lax.fori_loop(0, tracer_count // 2, functools.partial(group, True), 0)
+    @pl.loop(0, tracer_count // 2)
+    def _(pair):
+        group(True, [2 * pair, 2 * pair + 1])
 
     for m in range(3):
         speeds(m).wait_send()

time: 28.1 us -> 27.9 us (level)
  no operation moved by 1% of the time
where the time goes in v8:
time: 27.9 us; the launch traced here: 27.8 us
  Pallas kernels  27.8 us (100%)
    pallas_call x1, Pallas kernels, body(): pl.pallas_call(functools.partial(fused_kernel, lat_count, lon_count), out...  26.9 us
    pallas_call x1, Pallas kernels, body(): pl.pallas_call(deliver_kernel, out_shape=jax.ShapeDtypeStruct(tracers.sha...  0.89 us

profile of v8, /device:TPU:1, one launch (start us, length us, event | category | flops | bytes accessed | tf_op | source)
XLA Modules:
  0.0 27.8 jit_solution(13974744356017675084)
XLA Ops:
  0.0 26.9 %shard_map.109.held = f32[4,8,4,1440]{3,2,1,0:T(4,128)S(1)} custom-call(f32[4,8,4,1440]{3,2,1,0:T(4,128)} %tr.1, f32[8,4,1440]{2,1,0:T(4,128)} %cour.1, s32[4,8]{1,0:T(4,128)} %bitcast.4, f32[4,8]{1,0:T(4,128)} %bitcast.5, s32[2,128]{1,0:T(2,128)} %bitcast.6, f32[2,128]{1,0:T(2,128)} %bitcast.7, f32[2,23,128]{2,1,0:T(8,128)} %constant.10.clone.twid_in, ...), custom_call_target="tpu_custom_call" | custom-call | tf_op jit(solution)/shard_map/pallas_call | solution.py:534
  26.9 0.9 %shard_map.110 = f32[4,8,4,1440]{3,2,1,0:T(4,128)} custom-call(f32[4,8,4,1440]{3,2,1,0:T(4,128)S(1)} %shard_map.109.held), custom_call_target="tpu_custom_call" | custom-call | tf_op jit(solution)/shard_map/pallas_call | solution.py:563

commit v9 on v8

--- a/solution.py
+++ b/solution.py
@@ -164,10 +164,11 @@
     tr, cour, zs_in, zf_in, cut_in, damp_in,
     twid_in, kabs_in, scale_in, fwd_h_in, fwd_l_in, inv_h_in, inv_l_in,
     out,
-    got_t, got_c, halo_t, halo_c, parts,
+    got_t, got_c, halo_t, halo_c, parts, strips, joint, got_j,
     zs, zf, cut, damp, twid, kabs, scale, fwd_h, fwd_l, inv_h, inv_l,
     line, moved, spec, wave,
     t_send, t_recv, c_send, c_recv, h_send, h_recv, hc_send, hc_recv, b_send, b_recv, b_local, local, ready,
+    s_send, s_recv, s_local,
 ):
     tracer_count, _, row_count, columns = tr.shape
     lat = lax.axis_index("lat")
@@ -201,9 +202,23 @@
     first = pl.ds(0, 1)
     pieces = (pl.ds(1, row_count - 2), first, last)
 
+    whole = columns // LANES * LANES
+    spare = columns - whole
+    body = pl.ds(0, whole)
+    strip = pltpu.make_async_copy(
+        tr.at[:, :, :, pl.ds(whole, spare)], strips, s_local.at[0]
+    )
+    strip.start()
+
+    def ends(m):
+        return remote(
+            joint.at[levels[m]], got_j.at[lon], s_send.at[m], s_recv.at[m],
+            {"lat": lat, "lon": peers[m]},
+        )
+
     def cells(t, m, piece):
         return remote(
-            tr.at[t, levels[m], pieces[piece]], got_t.at[lon, t, :, pieces[piece]],
+            tr.at[t, levels[m], pieces[piece], body], got_t.at[lon, t, :, pieces[piece], body],
             t_send.at[t, 3 * m + piece], t_recv.at[t, 3 * m + piece],
             {"lat": lat, "lon": peers[m]},
         )
@@ -274,6 +289,11 @@
     pl.semaphore_wait(barrier, len(peers) + core * (2 * has_north + 2 * has_south))
     for m in (1, 2, 0):
         speeds(m).start()
+    strip.wait()
+    for level in range(tr.shape[1]):
+        joint[level] = jnp.concatenate([strips[t, level] for t in range(tracer_count)], axis=1)
+    for m in (1, 2, 0):
+        ends(m).start()
     for group_of in ((0,), (1,), (2, 3)):
         for piece in (1, 2, 0):
             for t in group_of:
@@ -468,6 +488,13 @@
             if edge:
                 keep(t).start()
 
+    for m in (0, 1, 2):
+        ends(m).wait_recv()
+        for level in range(2):
+            value = got_j[peers[m], level]
+            for t in range(tracer_count):
+                part = value if t == 0 else pltpu.roll(value, LANES - spare * t, 1)
+                got_t[peers[m], t, level, :, whole:columns] = part[:, :spare]
     for t in range(2):
         relay(t)
     group(False, [0, 1])
@@ -489,6 +516,7 @@
 
     for m in range(3):
         speeds(m).wait_send()
+        ends(m).wait_send()
 
     @pl.when(south_there)
     def _():
@@ -542,6 +570,9 @@
             pltpu.VMEM((lon_count, tracer_count) + tile, f32),
             pltpu.VMEM((lon_count,) + tile, f32),
             pltpu.VMEM((lon_count, tracer_count) + tile, f32),
+            pltpu.VMEM((tracer_count, level_count, row_count, columns % LANES), f32),
+            pltpu.VMEM((level_count, row_count, LANES), f32),
+            pltpu.VMEM((lon_count, per, row_count, LANES), f32),
             *small,
             pltpu.VMEM((8, columns * lon_count), f32),
             pltpu.VMEM((8, columns * lon_count), f32),
@@ -555,6 +586,7 @@
             dma((tracer_count,)),
             dma((len(operands),)),
             pltpu.SemaphoreType.REGULAR,
+            dma((3,)), dma((3,)), dma((1,)),
         ],
         compiler_params=pltpu.CompilerParams(
             collective_id=0, has_side_effects=True, vmem_limit_bytes=16 << 20

time: 27.9 us -> 27.5 us (0.986)
  Pallas kernels: 27.8 us -> 27.4 us
    pallas_call x1, Pallas kernels: 26.9 us -> 26.5 us  [body(): pl.pallas_call(functools.partial(fused_kernel, lat_count, lon_count), out...]
where the time goes in v9:
time: 27.5 us; the launch traced here: 27.4 us
  Pallas kernels  27.4 us (100%)
    pallas_call x1, Pallas kernels, body(): pl.pallas_call(functools.partial(fused_kernel, lat_count, lon_count), out...  26.5 us
    pallas_call x1, Pallas kernels, body(): pl.pallas_call(deliver_kernel, out_shape=jax.ShapeDtypeStruct(tracers.sha...  0.89 us

profile of v9, /device:TPU:1, one launch (start us, length us, event | category | flops | bytes accessed | tf_op | source)
XLA Modules:
  0.0 27.4 jit_solution(3374858537370988757)
XLA Ops:
  0.0 26.5 %shard_map.109.held = f32[4,8,4,1440]{3,2,1,0:T(4,128)S(1)} custom-call(f32[4,8,4,1440]{3,2,1,0:T(4,128)} %tr.1, f32[8,4,1440]{2,1,0:T(4,128)} %cour.1, s32[4,8]{1,0:T(4,128)} %bitcast.4, f32[4,8]{1,0:T(4,128)} %bitcast.5, s32[2,128]{1,0:T(2,128)} %bitcast.6, f32[2,128]{1,0:T(2,128)} %bitcast.7, f32[2,23,128]{2,1,0:T(8,128)} %constant.10.clone.twid_in, ...), custom_call_target="tpu_custom_call" | custom-call | tf_op jit(solution)/shard_map/pallas_call | solution.py:562
  26.5 0.9 %shard_map.110 = f32[4,8,4,1440]{3,2,1,0:T(4,128)} custom-call(f32[4,8,4,1440]{3,2,1,0:T(4,128)S(1)} %shard_map.109.held), custom_call_target="tpu_custom_call" | custom-call | tf_op jit(solution)/shard_map/pallas_call | solution.py:595

commit v10 on v9

--- a/solution.py
+++ b/solution.py
@@ -327,7 +327,7 @@
         for copy in rim_speeds()[:2]:
             copy.start()
 
-    for t in range(tracer_count):
+    for t in range(2):
         start_rims(rims(t)[:2])
     for copy in staged:
         copy.wait()
@@ -497,6 +497,7 @@
                 got_t[peers[m], t, level, :, whole:columns] = part[:, :spare]
     for t in range(2):
         relay(t)
+        start_rims(rims(t + 2)[:2])
     group(False, [0, 1])
     for t in range(2, tracer_count):
         relay(t)

time: 27.5 us -> 27.5 us (level)
  no operation moved by 1% of the time
where the time goes in v10:
time: 27.5 us; the launch traced here: 27.4 us
  Pallas kernels  27.4 us (100%)
    pallas_call x1, Pallas kernels, body(): pl.pallas_call(functools.partial(fused_kernel, lat_count, lon_count), out...  26.5 us
    pallas_call x1, Pallas kernels, body(): pl.pallas_call(deliver_kernel, out_shape=jax.ShapeDtypeStruct(tracers.sha...  0.89 us

profile of v10, /device:TPU:1, one launch (start us, length us, event | category | flops | bytes accessed | tf_op | source)
XLA Modules:
  0.0 27.4 jit_solution(16403531039620224733)
XLA Ops:
  0.0 26.5 %shard_map.109.held = f32[4,8,4,1440]{3,2,1,0:T(4,128)S(1)} custom-call(f32[4,8,4,1440]{3,2,1,0:T(4,128)} %tr.1, f32[8,4,1440]{2,1,0:T(4,128)} %cour.1, s32[4,8]{1,0:T(4,128)} %bitcast.4, f32[4,8]{1,0:T(4,128)} %bitcast.5, s32[2,128]{1,0:T(2,128)} %bitcast.6, f32[2,128]{1,0:T(2,128)} %bitcast.7, f32[2,23,128]{2,1,0:T(8,128)} %constant.10.clone.twid_in, ...), custom_call_target="tpu_custom_call" | custom-call | tf_op jit(solution)/shard_map/pallas_call | solution.py:563
  26.5 0.9 %shard_map.110 = f32[4,8,4,1440]{3,2,1,0:T(4,128)} custom-call(f32[4,8,4,1440]{3,2,1,0:T(4,128)S(1)} %shard_map.109.held), custom_call_target="tpu_custom_call" | custom-call | tf_op jit(solution)/shard_map/pallas_call | solution.py:596

commit v11 on v10

--- a/solution.py
+++ b/solution.py
@@ -189,8 +189,6 @@
     staged = [
         pltpu.make_async_copy(a, b, local.at[i]) for i, (a, b) in enumerate(staged)
     ]
-    for copy in staged:
-        copy.start()
 
     def remote(src, dst, send, recv, device):
         return pltpu.make_async_remote_copy(
@@ -208,7 +206,6 @@
     strip = pltpu.make_async_copy(
         tr.at[:, :, :, pl.ds(whole, spare)], strips, s_local.at[0]
     )
-    strip.start()
 
     def ends(m):
         return remote(
@@ -286,6 +283,9 @@
     keeper = peers[1] + 1 - core
     pl.when(north_there)(functools.partial(signal, {"lat": up, "lon": keeper}))
     pl.when(south_there)(functools.partial(signal, {"lat": down, "lon": keeper}))
+    strip.start()
+    for copy in staged:
+        copy.start()
     pl.semaphore_wait(barrier, len(peers) + core * (2 * has_north + 2 * has_south))
     for m in (1, 2, 0):
         speeds(m).start()

time: 27.5 us -> 27.5 us (level)
  no operation moved by 1% of the time
where the time goes in v11:
time: 27.5 us; the launch traced here: 27.4 us
  Pallas kernels  27.4 us (100%)
    pallas_call x1, Pallas kernels, body(): pl.pallas_call(functools.partial(fused_kernel, lat_count, lon_count), out...  26.5 us
    pallas_call x1, Pallas kernels, body(): pl.pallas_call(deliver_kernel, out_shape=jax.ShapeDtypeStruct(tracers.sha...  0.89 us

profile of v11, /device:TPU:1, one launch (start us, length us, event | category | flops | bytes accessed | tf_op | source)
XLA Modules:
  0.0 27.4 jit_solution(5656044691984960686)
XLA Ops:
  0.0 26.5 %shard_map.109.held = f32[4,8,4,1440]{3,2,1,0:T(4,128)S(1)} custom-call(f32[4,8,4,1440]{3,2,1,0:T(4,128)} %tr.1, f32[8,4,1440]{2,1,0:T(4,128)} %cour.1, s32[4,8]{1,0:T(4,128)} %bitcast.4, f32[4,8]{1,0:T(4,128)} %bitcast.5, s32[2,128]{1,0:T(2,128)} %bitcast.6, f32[2,128]{1,0:T(2,128)} %bitcast.7, f32[2,23,128]{2,1,0:T(8,128)} %constant.10.clone.twid_in, ...), custom_call_target="tpu_custom_call" | custom-call | tf_op jit(solution)/shard_map/pallas_call | solution.py:563
  26.5 0.9 %shard_map.110 = f32[4,8,4,1440]{3,2,1,0:T(4,128)} custom-call(f32[4,8,4,1440]{3,2,1,0:T(4,128)S(1)} %shard_map.109.held), custom_call_target="tpu_custom_call" | custom-call | tf_op jit(solution)/shard_map/pallas_call | solution.py:596

commit v12 on v11

--- a/solution.py
+++ b/solution.py
@@ -277,12 +277,12 @@
     def signal(friend):
         pl.semaphore_signal(barrier, inc=1, device_id=friend, device_id_type=MESH)
 
-    for peer in peers:
-        signal({"lat": lat, "lon": peer})
     core = lax.rem(lon, 2)
     keeper = peers[1] + 1 - core
     pl.when(north_there)(functools.partial(signal, {"lat": up, "lon": keeper}))
     pl.when(south_there)(functools.partial(signal, {"lat": down, "lon": keeper}))
+    for peer in peers:
+        signal({"lat": lat, "lon": peer})
     strip.start()
     for copy in staged:
         copy.start()

time: 27.5 us -> 27.5 us (level)
  no operation moved by 1% of the time
where the time goes in v12:
time: 27.5 us; the launch traced here: 27.4 us
  Pallas kernels  27.4 us (100%)
    pallas_call x1, Pallas kernels, body(): pl.pallas_call(functools.partial(fused_kernel, lat_count, lon_count), out...  26.5 us
    pallas_call x1, Pallas kernels, body(): pl.pallas_call(deliver_kernel, out_shape=jax.ShapeDtypeStruct(tracers.sha...  0.89 us

profile of v12, /device:TPU:1, one launch (start us, length us, event | category | flops | bytes accessed | tf_op | source)
XLA Modules:
  0.0 27.4 jit_solution(10454908442251141120)
XLA Ops:
  0.0 26.5 %shard_map.109.held = f32[4,8,4,1440]{3,2,1,0:T(4,128)S(1)} custom-call(f32[4,8,4,1440]{3,2,1,0:T(4,128)} %tr.1, f32[8,4,1440]{2,1,0:T(4,128)} %cour.1, s32[4,8]{1,0:T(4,128)} %bitcast.4, f32[4,8]{1,0:T(4,128)} %bitcast.5, s32[2,128]{1,0:T(2,128)} %bitcast.6, f32[2,128]{1,0:T(2,128)} %bitcast.7, f32[2,23,128]{2,1,0:T(8,128)} %constant.10.clone.twid_in, ...), custom_call_target="tpu_custom_call" | custom-call | tf_op jit(solution)/shard_map/pallas_call | solution.py:563
  26.5 0.9 %shard_map.110 = f32[4,8,4,1440]{3,2,1,0:T(4,128)} custom-call(f32[4,8,4,1440]{3,2,1,0:T(4,128)S(1)} %shard_map.109.held), custom_call_target="tpu_custom_call" | custom-call | tf_op jit(solution)/shard_map/pallas_call | solution.py:596
